TPU v7x, 256 devices: a whole 4x4x8 slice. The times are simulated.
256 devices in a mesh: dp: 4 (over y), expert: 64 (over x, z, core).
Axes of the slice: x: 4, y: 4, z: 8, core: 2. Of those that a mesh axis runs over, the one named last changes fastest.
Arguments:
- tokens: bfloat16 [32768, 2048], P(('dp', 'expert')), may hold values from -6 to 6
- expert_ids: int32 [32768, 3], P(('dp', 'expert')), may hold values from 0 to 63, all different within a row; in each aligned block of 128 rows (0 to 127, 128 to 255, ...) at most 8 rows name the same one
- gate_level: int32 [32768, 3], P(('dp', 'expert')), may hold values from 0 to 15
- cost_bucket: int32 [512], P(('dp', 'expert')), may hold values from 0 to 7
- gate_table: float32 [8, 16], replicated, may hold values from 0.05 to 0.6
- gate_weight: bfloat16 [64, 2048, 768], P('expert', 'dp'), may hold values from -0.125 to 0.125
- up_weight: bfloat16 [64, 2048, 768], P('expert', 'dp'), may hold values from -0.125 to 0.125
- down_weight: bfloat16 [64, 2048, 768], P('expert', 'dp'), may hold values from -0.21875 to 0.21875
- out_grad: bfloat16 [32768, 2048], P(('dp', 'expert')), may hold values from -6 to 6
Outputs:
- output: bfloat16 [32768, 2048], P(('dp', 'expert'))
- token_grad: bfloat16 [32768, 2048], P(('dp', 'expert'))
- gate_grad: float32 [64, 2048, 768], P('expert', 'dp')
- up_grad: float32 [64, 2048, 768], P('expert', 'dp')
- down_grad: float32 [64, 2048, 768], P('expert', 'dp')
Inputs may be any that keep to these rules, and one draw needn't show every extreme that they name: `expert_ids`: each row names 3 different experts. Among the rows of one device (aligned blocks of 128 rows) no expert is named more than 8 times, and in every draw some expert is named exactly 8 times in some block.
All inputs are finite; a program needn't handle non-finite values.
Results may differ from a plain program's by a relative error of at most 0.0085.
Values may be sent and summed in bfloat16 or wider, within the bound.
No kernel may reach another device: no remote copies, remote signals or barrier semaphores. Data moves between devices by JAX's collectives and lax.ppermute only.
A program may use at most 128 MiB of HBM per device.

v0:
```python
import functools

import jax
import jax.numpy as jnp
from jax import lax
from jax.experimental import pallas as pl
from jax.experimental.pallas import tpu as pltpu
from jax.sharding import PartitionSpec as P


BF = jnp.bfloat16
F32 = jnp.float32
FIRST = (((0,), (0,)), ((), ()))
LAST = (((1,), (1,)), ((), ()))
VMEM = pl.BlockSpec(memory_space=pltpu.VMEM)
SMEM = pl.BlockSpec(memory_space=pltpu.SMEM)
LIMIT = 67_043_328


def shape_of(shape, dtype):
    return jax.ShapeDtypeStruct(shape, dtype)


def whole(kernel, outs, n_in, flops=0, nbytes=0, smem=()):
    call = pl.pallas_call(
        kernel,
        out_shape=outs,
        in_specs=[SMEM if i in smem else VMEM for i in range(n_in)],
        out_specs=[VMEM for _ in outs],
        compiler_params=pltpu.CompilerParams(vmem_limit_bytes=LIMIT),
        cost_estimate=pl.CostEstimate(flops=flops, bytes_accessed=nbytes, transcendentals=0),
    )
    return call


def chosen(place, slots):
    spots = lax.broadcasted_iota(jnp.int32, (slots, place.shape[1]), 0)
    return [place[k : k + 1, :] == spots for k in range(place.shape[0])]


def added(terms):
    total = terms[0]
    for term in terms[1:]:
        total = total + term
    return total


def send_kernel(members, capacity, ids_ref, tokens_ref, rows_ref, place_ref):
    top, count = ids_ref.shape
    names = lax.broadcasted_iota(jnp.int32, (members, count), 0)
    before = (
        lax.broadcasted_iota(jnp.int32, (count, count), 0)
        < lax.broadcasted_iota(jnp.int32, (count, count), 1)
    ).astype(BF)
    ahead = jnp.zeros((members, 1), F32)
    places = []
    for k in range(top):
        ids = ids_ref[k : k + 1, :]
        hot = (ids == names).astype(F32)
        earlier = jnp.dot(hot.astype(BF), before, preferred_element_type=F32) + ahead
        rank = jnp.sum(hot * earlier, axis=0, keepdims=True).astype(jnp.int32)
        ahead = ahead + jnp.sum(hot, axis=1, keepdims=True)
        places.append(ids * capacity + rank)
        place_ref[k : k + 1, :] = places[-1]
    spots = lax.broadcasted_iota(jnp.int32, (members * capacity, count), 0)
    pick = added([(place == spots).astype(F32) for place in places]).astype(BF)
    rows_ref[...] = jnp.dot(pick, tokens_ref[...], preferred_element_type=F32).astype(BF)


def grad_send_kernel(bucket_ref, table_ref, place_ref, level_ref, grad_ref, rows_ref, gate_ref):
    top, count = place_ref.shape
    slots = rows_ref.shape[0]
    trajs = bucket_ref.shape[0]
    level = level_ref[...]
    traj = lax.broadcasted_iota(jnp.int32, (top, count), 1) // (count // trajs)
    gate = jnp.zeros((top, count), F32)
    for at in range(table_ref.shape[1]):
        entry = jnp.zeros((top, count), F32)
        for j in range(trajs):
            entry = jnp.where(traj == j, table_ref[bucket_ref[j], at], entry)
        gate = jnp.where(level == at, entry, gate)
    gate_ref[...] = gate
    hots = chosen(place_ref[...], slots)
    pick = added([hot.astype(F32) for hot in hots]).astype(BF)
    gated = added([jnp.where(hot, gate[k : k + 1, :], 0.0) for k, hot in enumerate(hots)])
    slot_gate = jnp.sum(gated, axis=1, keepdims=True)
    rows = jnp.dot(pick, grad_ref[...], preferred_element_type=F32)
    rows_ref[...] = (rows * slot_gate).astype(BF)


def pick_kernel(place_ref, gate_ref, pick_ref, gated_ref):
    hots = chosen(place_ref[...], pick_ref.shape[1])
    pick_ref[...] = added([hot.astype(F32) for hot in hots]).T.astype(BF)
    gate = gate_ref[...]
    gated_ref[...] = added(
        [jnp.where(hot, gate[k : k + 1, :], 0.0) for k, hot in enumerate(hots)]
    ).T


def split_kernel(gated_ref, pieces_ref):
    rest = gated_ref[...]
    for i in range(pieces_ref.shape[0]):
        piece = rest.astype(BF)
        pieces_ref[i] = piece
        rest = rest - piece.astype(F32)


def columns(offset, size):
    return pl.ds(pl.multiple_of(offset, 128), size)


def offsets(y, n, size):
    at = lambda j: lax.rem(y + j, n) * size
    half = size // 2
    return [(at(0), size), (at(3), size), (at(1), size), (at(2), half), (at(2) + half, half)]


def forward_kernel(y_ref, rows_ref, *refs):
    gates, ups, (ga_ref, ua_ref, hid_ref) = refs[0:5], refs[5:10], refs[10:]
    gate_act = up_act = None
    for (off, size), g, u in zip(offsets(y_ref[0], 4, gates[0].shape[0]), gates, ups):
        rows = rows_ref[:, columns(off, size)]
        a = jnp.dot(rows, g[...], preferred_element_type=F32)
        b = jnp.dot(rows, u[...], preferred_element_type=F32)
        gate_act = a if gate_act is None else gate_act + a
        up_act = b if up_act is None else up_act + b
    ga_ref[...] = gate_act
    ua_ref[...] = up_act
    hid_ref[...] = (gate_act * jax.nn.sigmoid(gate_act) * up_act).astype(BF)


def backward_kernel(y_ref, rows_ref, *refs):
    downs, (ga_ref, ua_ref, gg_ref, gu_ref) = refs[0:5], refs[5:]
    grad = None
    for (off, size), d in zip(offsets(y_ref[0], 4, downs[0].shape[0]), downs):
        a = jnp.dot(rows_ref[:, columns(off, size)], d[...], preferred_element_type=F32)
        grad = a if grad is None else grad + a
    gate_act = ga_ref[...]
    s = jax.nn.sigmoid(gate_act)
    gg_ref[...] = (grad * ua_ref[...] * s * (1.0 + gate_act * (1.0 - s))).astype(BF)
    gu_ref[...] = (grad * (gate_act * s)).astype(BF)


def by_hidden(kernel, y, rows, weights, acts, outs, tile):
    depth, hidden = rows.shape[0], weights[0][0].shape[2]
    act = pl.BlockSpec((depth, tile), lambda h, y_ref: (0, h))
    specs = [pl.BlockSpec(rows.shape, lambda h, y_ref: (0, 0))]
    for w, i in weights:
        specs.append(
            pl.BlockSpec((None, w.shape[1], tile), lambda h, y_ref, i=i: (i, 0, h))
        )
    specs += [act] * len(acts)
    size = sum(w.shape[1] * w.shape[2] for w, _ in weights)
    call = pl.pallas_call(
        kernel,
        grid_spec=pltpu.PrefetchScalarGridSpec(
            num_scalar_prefetch=1,
            grid=(hidden // tile,),
            in_specs=specs,
            out_specs=[act] * len(outs),
        ),
        out_shape=[shape_of((depth, hidden), d) for d in outs],
        compiler_params=pltpu.CompilerParams(vmem_limit_bytes=LIMIT),
        cost_estimate=pl.CostEstimate(
            flops=2 * depth * size,
            bytes_accessed=2 * (rows.size + size) + 8 * depth * hidden,
            transcendentals=0,
        ),
    )
    return call(y, rows, *[w for w, _ in weights], *acts)


def spread_kernel(groups, y_ref, *refs):
    acts, out_ref = refs[:groups], refs[-1]
    weights = [refs[groups + 5 * i : groups + 5 * i + 5] for i in range(groups)]
    for j, (off, size) in enumerate(offsets(y_ref[0], 4, weights[0][0].shape[0])):
        total = None
        for a, w in zip(acts, weights):
            part = lax.dot_general(a[...], w[j][...], LAST, preferred_element_type=F32)
            total = part if total is None else total + part
        out_ref[:, columns(off, size)] = total.astype(BF)


def spread(y, acts, weights):
    depth, hidden = acts[0].shape
    width = 4 * weights[0][0][0].shape[1]
    flat = [w for ws in weights for w in ws]
    act = pl.BlockSpec((depth, hidden), lambda g, y_ref: (0, 0))
    call = pl.pallas_call(
        functools.partial(spread_kernel, len(acts)),
        grid_spec=pltpu.PrefetchScalarGridSpec(
            num_scalar_prefetch=1,
            grid=(1,),
            in_specs=[act] * len(acts)
            + [
                pl.BlockSpec((None, w.shape[1], hidden), lambda g, y_ref, i=i: (i, 0, 0))
                for w, i in flat
            ],
            out_specs=pl.BlockSpec((depth, width), lambda g, y_ref: (0, 0)),
        ),
        out_shape=shape_of((depth, width), BF),
        compiler_params=pltpu.CompilerParams(vmem_limit_bytes=LIMIT),
        cost_estimate=pl.CostEstimate(
            flops=2 * depth * width * hidden * len(acts),
            bytes_accessed=2 * width * (depth + hidden * len(acts)),
            transcendentals=0,
        ),
    )
    return call(y, *acts, *[w for w, _ in flat])


def partial_kernel(parts, y_ref, rows_ref, *refs):
    acts, (own_ref, up_ref, dn_ref, up_a, dn_b) = refs[:parts], refs[parts:]
    size = own_ref.shape[0]
    half = size // 2
    y = y_ref[0]
    spots = [(2, 0, up_ref, 0, half), (1, half, up_ref, half, half)]
    spots += [(2, half, dn_ref, 0, half), (3, 0, dn_ref, half, half)]
    spots += [(1, 0, up_a, 0, half), (3, half, dn_b, 0, half), (0, 0, own_ref, 0, size)]
    for j, lead, ref, top, length in spots:
        rows = rows_ref[:, columns(lax.rem(y + j, 4) * size + lead, length)]
        at = 0
        for a in acts:
            ref[top : top + length, at : at + a.shape[1]] = lax.dot_general(
                rows, a[...], FIRST, preferred_element_type=F32
            ).astype(BF)
            at += a.shape[1]


def partials(y, rows, acts, size):
    wide = sum(a.shape[1] for a in acts)
    full, half = shape_of((size, wide), BF), shape_of((size // 2, wide), BF)
    return whole(
        functools.partial(partial_kernel, len(acts)),
        [full, full, full, half, half],
        2 + len(acts),
        flops=2 * rows.size * wide,
        nbytes=2 * (rows.size + 4 * size * wide),
        smem=(0,),
    )(y, rows, *acts)


def sum_kernel(own_ref, up_ref, dn_ref, below_ref, above_ref, *outs):
    half = below_ref.shape[0]
    hidden = outs[0].shape[2]
    for i, out in enumerate(outs):
        at = slice(i * hidden, (i + 1) * hidden)
        out[0, :half] = (
            own_ref[:half, at].astype(F32)
            + below_ref[:, at].astype(F32)
            + dn_ref[half:, at].astype(F32)
        )
        out[0, half:] = (
            own_ref[half:, at].astype(F32)
            + up_ref[half:, at].astype(F32)
            + above_ref[:, at].astype(F32)
        )


def output_kernel(pieces_ref, rows_ref, out_ref):
    rows = rows_ref[...]
    out_ref[...] = added(
        [
            jnp.dot(pieces_ref[i], rows, preferred_element_type=F32)
            for i in range(pieces_ref.shape[0])
        ]
    ).astype(BF)


def token_grad_kernel(pick_ref, rows_ref, out_ref):
    out_ref[...] = jnp.dot(pick_ref[...], rows_ref[...], preferred_element_type=F32).astype(BF)


def move_rows(rows, members):
    depth, width = rows.shape
    buffer = rows.reshape(members, depth // members, width)
    moved = lax.all_to_all(buffer, "expert", split_axis=0, concat_axis=0, tiled=True)
    return moved.reshape(depth, width)


def shift(x, by):
    return lax.ppermute(x, "dp", [(i, (i + by) % 4) for i in range(4)])


def ring_gather(weights):
    shard = jnp.concatenate(weights, axis=0)
    half = shard.shape[1] // 2
    below, above = shift(shard, 1), shift(shard, -1)
    far_a = shift(below[:, :half], 1)
    far_b = shift(above[:, half:], -1)
    return [
        [(w, 0), (below, i), (above, i), (far_a, i), (far_b, i)] for i, w in enumerate(weights)
    ]


def ring_sum(parts, own, up, dn, up_a, dn_b):
    size, wide = own.shape
    half = size // 2
    got_up, got_dn = shift(up, 1), shift(dn, -1)
    up_a = (up_a.astype(F32) + got_up[:half].astype(F32)).astype(BF)
    dn_b = (dn_b.astype(F32) + got_dn[:half].astype(F32)).astype(BF)
    below, above = shift(up_a, 1), shift(dn_b, -1)
    return whole(
        sum_kernel, [shape_of((1, size, wide // parts), F32)] * parts, 5, nbytes=12 * size * wide
    )(own, got_up, got_dn, below, above)


def shards(
    tokens,
    expert_ids,
    gate_level,
    cost_bucket,
    gate_table,
    gate_weight,
    up_weight,
    down_weight,
    out_grad,
):
    count, width = tokens.shape
    top = expert_ids.shape[1]
    members = lax.axis_size("expert")
    capacity = min(count, 4 * count * top // (3 * members))
    slots = members * capacity
    size, _ = gate_weight.shape[1:]
    y = lax.axis_index("dp").astype(jnp.int32).reshape(1)

    rows, place = whole(
        functools.partial(send_kernel, members, capacity),
        [shape_of((slots, width), BF), shape_of((top, count), jnp.int32)],
        2,
        nbytes=3 * 2**20,
    )(expert_ids.T, tokens)
    expert_rows = move_rows(rows, members)
    g_rows, gates = whole(
        grad_send_kernel,
        [shape_of((slots, width), BF), shape_of((top, count), F32)],
        5,
        nbytes=3 * 2**20,
        smem=(0, 1),
    )(cost_bucket, gate_table, place, gate_level.T, out_grad)
    grad_rows = move_rows(g_rows, members)
    pick, gated = whole(
        pick_kernel, [shape_of((count, slots), BF), shape_of((count, slots), F32)], 2, nbytes=2**20
    )(place, gates)
    pieces = whole(split_kernel, [shape_of((3, count, slots), BF)], 1, nbytes=2**20)(gated)[0]

    w_gate, w_up, w_down = ring_gather([gate_weight, up_weight, down_weight])
    gate_act, up_act, hid = by_hidden(
        forward_kernel, y, expert_rows, w_gate + w_up, [], [F32, F32, BF], 256
    )
    result = spread(y, [hid], [w_down])
    returned = move_rows(result, members)

    grad_gate, grad_up = by_hidden(
        backward_kernel, y, grad_rows, w_down, [gate_act, up_act], [BF, BF], 256
    )
    grad_in = spread(y, [grad_gate, grad_up], [w_gate, w_up])
    grad_back = move_rows(grad_in, members)
    output = whole(output_kernel, [shape_of((count, width), BF)], 2, nbytes=3 * 2**20)(
        pieces, returned
    )[0]
    token_grad = whole(
        token_grad_kernel, [shape_of((count, width), BF)], 2, nbytes=3 * 2**20
    )(pick, grad_back)[0]

    down_grad = ring_sum(1, *partials(y, grad_rows, [hid], size))[0]
    gate_grad, up_grad = ring_sum(2, *partials(y, expert_rows, [grad_gate, grad_up], size))
    return (output, token_grad, gate_grad, up_grad, down_grad)


def solution(mesh):
    both = ("dp", "expert")
    return jax.shard_map(
        shards,
        mesh=mesh,
        in_specs=(
            P(both, None),
            P(both, None),
            P(both, None),
            P(both),
            P(),
            P("expert", "dp", None),
            P("expert", "dp", None),
            P("expert", "dp", None),
            P(both, None),
        ),
        out_specs=(
            P(both, None),
            P(both, None),
            P("expert", "dp", None),
            P("expert", "dp", None),
            P("expert", "dp", None),
        ),
        check_vma=False,
    )
```

profile of v0, /device:TPU:1, one launch (start us, length us, event | category | flops | bytes accessed | tf_op | source)
XLA Modules:
  0.0 343.1 jit_solution(6564146507242825925)
XLA Ops:
  0.6 3.3 shard_map.128
  4.0 13.2 %all-to-all-start = ((bf16[64,8,2048]{2,1,0:T(8,128)(2,1)}), bf16[64,8,2048]{2,1,0:T(8,128)(2,1)}, u32[]{:S(2)}, u32[]{:S(2)}) async-start(bf16[64,8,2048]{2,1,0:T(8,128)(2,1)} %bitcast.14), calls=%async_computation | async-start | bytes 4194304 | tf_op jit(solution)/shard_map/all_to_all | solution.py:277
  17.1 3.2 shard_map.129
  20.4 1.2 constant_dynamic-update-slice_fusion.2
  21.6 46.7 %all-to-all-done = bf16[64,8,2048]{2,1,0:T(8,128)(2,1)} async-done(((bf16[64,8,2048]{2,1,0:T(8,128)(2,1)}), bf16[64,8,2048]{2,1,0:T(8,128)(2,1)}, u32[]{:S(2)}, u32[]{:S(2)}) %all-to-all-start) | async-done | bytes 2097184 | tf_op jit(solution)/shard_map/all_to_all | solution.py:277
  68.2 6.2 %all-to-all-start.2 = ((bf16[64,8,2048]{2,1,0:T(8,128)(2,1)}), bf16[64,8,2048]{2,1,0:T(8,128)(2,1)}, u32[]{:S(2)}, u32[]{:S(2)}) async-start(bf16[64,8,2048]{2,1,0:T(8,128)(2,1)} %bitcast.13), calls=%async_computation.2 | async-start | bytes 4194304 | tf_op jit(solution)/shard_map/all_to_all | solution.py:277
  74.4 0.0 copy-done.2
  74.4 0.0 copy-start.3
  74.4 0.1 constant_dynamic-update-slice_fusion.1
  74.5 1.1 copy-done.3
  75.6 0.1 constant_dynamic-update-slice_fusion
  75.6 2.8 collective-permute-start.1
  78.4 0.0 collective-permute-start
  78.4 50.1 %collective-permute-done.1.refs_2_.refs_7_.refs_3_.refs_4_.refs_9_ = bf16[3,512,768]{2,1,0:T(8,128)(2,1)S(1)} collective-permute-done((bf16[3,512,768]{2,1,0:T(8,128)(2,1)S(1)}, bf16[3,512,768]{2,1,0:T(8,128)(2,1)S(1)}, u32[]{:S(2)}, u32[]{:S(2)}) %collective-permute-start.1) | collective-permute-done | bytes 2359328 | tf_op jit(solution)/shard_map/ppermute | solution.py:282
  128.5 0.1 slice.25
  128.6 3.5 %collective-permute-start.3 = (bf16[3,256,768]{2,1,0:T(8,128)(2,1)S(1)}, bf16[3,256,768]{2,1,0:T(8,128)(2,1)}, u32[]{:S(2)}, u32[]{:S(2)}) collective-permute-start(bf16[3,256,768]{2,1,0:T(8,128)(2,1)S(1)} %slice.25), channel_id=1, source_target_pairs={{0,192},{64,0},{128,64},{192,128},{1,193},{65,1},{129,65},{193,129... | collective-permute-start | bytes 3538952 | tf_op jit(solution)/shard_map/ppermute | solution.py:282
  132.1 0.0 collective-permute-done.refs_1_.refs_6_.refs_2_.refs_3_.refs_8_
  132.1 0.1 slice.24
  132.2 0.0 copy-done
  132.2 0.1 collective-permute-start.2
  132.3 1.2 copy-done.1
  133.5 22.5 %collective-permute-done.3.refs_4_.refs_9_.refs_5_.refs_6_.refs_11_ = bf16[3,256,768]{2,1,0:T(8,128)(2,1)} collective-permute-done((bf16[3,256,768]{2,1,0:T(8,128)(2,1)S(1)}, bf16[3,256,768]{2,1,0:T(8,128)(2,1)}, u32[]{:S(2)}, u32[]{:S(2)}) %collective-permute-start.3) | collective-permute-done | bytes 1179680 | tf_op jit(solution)/shard_map/ppermute | solution.py:282
  156.0 3.4 collective-permute-done.2.refs_3_.refs_8_.refs_4_.refs_5_.refs_10_
  159.4 8.4 %shard_map.132 = (f32[512,768]{1,0:T(8,128)}, f32[512,768]{1,0:T(8,128)}, bf16[512,768]{1,0:T(8,128)(2,1)}) custom-call(s32[1]{0:T(128)} %bitcast.2.y_ref, bf16[512,2048]{1,0:T(8,128)(2,1)} %bitcast.4.rows_ref, bf16[1,512,768]{2,1,0:T(8,128)(2,1)} %refs_2_.1, bf16[3,512,768]{2,1,0:T(8,128)(2,1)} %copy-done.1, bf16[3,512,768]{2,1,0:T(8,128)(2,1)} %copy-done, ...), custom_call_target="tpu_custom_call" | custom-call | flops 3221225472 | bytes 11534336 | tf_op jit(solution)/shard_map/pallas_call | solution.py:170
  167.8 5.2 %shard_map.133 = bf16[512,2048]{1,0:T(8,128)(2,1)} custom-call(s32[1]{0:T(128)} %bitcast.2.y_ref, bf16[512,768]{1,0:T(8,128)(2,1)} %get-tuple-element.32.refs_0_, bf16[1,512,768]{2,1,0:T(8,128)(2,1)} %refs_0_.3, bf16[3,512,768]{2,1,0:T(8,128)(2,1)} %copy-done.1, bf16[3,512,768]{2,1,0:T(8,128)(2,1)} %copy-done, ...), custom_call_target="tpu_custom_call" | custom-call | flops 1610612736 | bytes 5242880 | tf_op jit(solution)/shard_map/pallas_call | solution.py:209
  173.0 0.0 all-to-all-done.2
  173.0 12.8 %all-to-all-start.1 = ((bf16[64,8,2048]{2,1,0:T(8,128)(2,1)}), bf16[64,8,2048]{2,1,0:T(8,128)(2,1)}, u32[]{:S(2)}, u32[]{:S(2)}) async-start(bf16[64,8,2048]{2,1,0:T(8,128)(2,1)} %bitcast.11), calls=%async_computation.1 | async-start | bytes 4194304 | tf_op jit(solution)/shard_map/all_to_all | solution.py:277
  185.8 7.0 %shard_map.135 = (bf16[512,768]{1,0:T(8,128)(2,1)}, bf16[512,768]{1,0:T(8,128)(2,1)}) custom-call(s32[1]{0:T(128)} %bitcast.2.y_ref, bf16[512,2048]{1,0:T(8,128)(2,1)} %bitcast.8.rows_ref, bf16[1,512,768]{2,1,0:T(8,128)(2,1)} %refs_0_.3, bf16[3,512,768]{2,1,0:T(8,128)(2,1)} %copy-done.1, bf16[3,512,768]{2,1,0:T(8,128)(2,1)} %copy-done, ...), custom_call_target="tpu_custom_call" | custom-call | flops 1610612736 | bytes 8388608 | tf_op jit(solution)/shard_map/pallas_call | solution.py:170
  192.9 8.0 %shard_map.136 = bf16[512,2048]{1,0:T(8,128)(2,1)} custom-call(s32[1]{0:T(128)} %bitcast.2.y_ref, bf16[512,768]{1,0:T(8,128)(2,1)} %get-tuple-element.37.refs_0_, bf16[512,768]{1,0:T(8,128)(2,1)} %get-tuple-element.38.refs_1_, bf16[1,512,768]{2,1,0:T(8,128)(2,1)} %refs_2_.1, bf16[3,512,768]{2,1,0:T(8,128)(2,1)} %copy-done.1, bf16[3,512,768]{2,1,0:T(8,128)(2,1)} %copy-done, ...), custom_call_target="tpu_custom_call" | custom-call | flops 3221225472 | bytes 8388608 | tf_op jit(solution)/shard_map/pallas_call | solution.py:209
  200.9 36.1 %all-to-all-done.1 = bf16[64,8,2048]{2,1,0:T(8,128)(2,1)} async-done(((bf16[64,8,2048]{2,1,0:T(8,128)(2,1)}), bf16[64,8,2048]{2,1,0:T(8,128)(2,1)}, u32[]{:S(2)}, u32[]{:S(2)}) %all-to-all-start.1) | async-done | bytes 2097184 | tf_op jit(solution)/shard_map/all_to_all | solution.py:277
  236.9 6.0 %all-to-all-start.3 = ((bf16[64,8,2048]{2,1,0:T(8,128)(2,1)}), bf16[64,8,2048]{2,1,0:T(8,128)(2,1)}, u32[]{:S(2)}, u32[]{:S(2)}) async-start(bf16[64,8,2048]{2,1,0:T(8,128)(2,1)} %bitcast.12), calls=%async_computation.3 | async-start | bytes 4194304 | tf_op jit(solution)/shard_map/all_to_all | solution.py:277
  243.0 6.6 %shard_map.138 = (bf16[512,1536]{1,0:T(8,128)(2,1)}, bf16[512,1536]{1,0:T(8,128)(2,1)}, bf16[512,1536]{1,0:T(8,128)(2,1)}, bf16[256,1536]{1,0:T(8,128)(2,1)}, bf16[256,1536]{1,0:T(8,128)(2,1)}) custom-call(s32[1]{0:T(128)} %bitcast.2.y_ref, bf16[512,2048]{1,0:T(8,128)(2,1)} %bitcast.4.rows_ref, bf16[512,768]{1,0:T(8,128)(2,1)} %get-tuple-element.37.refs_0_, ...), custom_call_target="tpu_custom_call" | custom-call | flops 3221225472 | bytes 8388608 | tf_op jit(solution)/shard_map/pallas_call | solution.py:233
  249.6 0.0 collective-permute-start.4
  249.6 2.7 collective-permute-start.5
  252.3 4.5 %shard_map.140 = (bf16[512,768]{1,0:T(8,128)(2,1)}, bf16[512,768]{1,0:T(8,128)(2,1)}, bf16[512,768]{1,0:T(8,128)(2,1)}, bf16[256,768]{1,0:T(8,128)(2,1)}, bf16[256,768]{1,0:T(8,128)(2,1)}) custom-call(s32[1]{0:T(128)} %bitcast.2.y_ref, bf16[512,2048]{1,0:T(8,128)(2,1)} %bitcast.8.rows_ref, bf16[512,768]{1,0:T(8,128)(2,1)} %get-tuple-element.32.refs_0_), custom_call_target="tpu_custom_call" | custom-call | flops 1610612736 | bytes 5242880 | tf_op jit(solution)/shard_map/pallas_call | solution.py:233
  256.8 0.0 collective-permute-start.8
  256.8 2.7 collective-permute-start.9
  259.5 27.1 %collective-permute-done.4.up_ref = bf16[512,1536]{1,0:T(8,128)(2,1)} collective-permute-done((bf16[512,1536]{1,0:T(8,128)(2,1)}, bf16[512,1536]{1,0:T(8,128)(2,1)}, u32[]{:S(2)}, u32[]{:S(2)}) %collective-permute-start.4) | collective-permute-done | bytes 1572896 | tf_op jit(solution)/shard_map/ppermute | solution.py:282
  286.6 2.4 add_convert_fusion.1
  289.0 0.0 collective-permute-start.6
  289.0 0.0 collective-permute-done.5.dn_ref
  289.0 0.0 copy-done.6
  289.0 0.0 copy-start.7
  289.0 2.3 add_convert_fusion
  291.3 2.6 collective-permute-start.7
  293.9 9.4 %collective-permute-done.8.up_ref = bf16[512,768]{1,0:T(8,128)(2,1)S(1)} collective-permute-done((bf16[512,768]{1,0:T(8,128)(2,1)}, bf16[512,768]{1,0:T(8,128)(2,1)S(1)}, u32[]{:S(2)}, u32[]{:S(2)}) %collective-permute-start.8) | collective-permute-done | bytes 786464 | tf_op jit(solution)/shard_map/ppermute | solution.py:282
  303.3 0.9 copy-done.4
  304.2 0.8 add_convert_fusion.3
  305.0 0.0 collective-permute-start.10
  305.0 0.0 collective-permute-done.9.dn_ref
  305.1 0.9 copy-done.5
  305.9 0.8 add_convert_fusion.2
  306.8 2.7 collective-permute-start.11
  309.5 1.7 shard_map.130
  311.1 1.8 shard_map.131.pieces_ref
  312.9 15.8 %collective-permute-done.10.below_ref = bf16[256,768]{1,0:T(8,128)(2,1)} collective-permute-done((bf16[256,768]{1,0:T(8,128)(2,1)}, bf16[256,768]{1,0:T(8,128)(2,1)}, u32[]{:S(2)}, u32[]{:S(2)}) %collective-permute-start.10) | collective-permute-done | bytes 393248 | tf_op jit(solution)/shard_map/ppermute | solution.py:282
  328.7 0.0 collective-permute-done.11.above_ref
  328.7 3.2 shard_map.141
  331.9 0.0 collective-permute-done.6.below_ref
  331.9 0.0 collective-permute-done.7.above_ref
  331.9 4.7 %shard_map.139 = (f32[1,512,768]{2,1,0:T(8,128)}, f32[1,512,768]{2,1,0:T(8,128)}) custom-call(bf16[512,1536]{1,0:T(8,128)(2,1)} %get-tuple-element.39.own_ref, bf16[512,1536]{1,0:T(8,128)(2,1)} %collective-permute-done.4.up_ref, bf16[512,1536]{1,0:T(8,128)(2,1)} %collective-permute-done.5.dn_ref, bf16[256,1536]{1,0:T(8,128)(2,1)} %collective-permute-done.6.below_ref, ...), custom_call_target="tpu_custom_call" | custom-call | bytes 9437184 | tf_op jit(solution)/shard_map/pallas_call | solution.py:303
  336.6 3.5 %shard_map.134 = bf16[128,2048]{1,0:T(8,128)(2,1)} custom-call(bf16[3,128,512]{2,1,0:T(8,128)(2,1)} %shard_map.131.pieces_ref, bf16[512,2048]{1,0:T(8,128)(2,1)} %bitcast.6.rows_ref), custom_call_target="tpu_custom_call" | custom-call | bytes 3145728 | tf_op jit(solution)/shard_map/pallas_call | solution.py:359
  340.2 0.0 all-to-all-done.3
  340.2 2.9 shard_map.137
  (9 shorter events, 0.0 us)
Async XLA Ops:
  4.0 64.3 %all-to-all-start = ((bf16[64,8,2048]{2,1,0:T(8,128)(2,1)}), bf16[64,8,2048]{2,1,0:T(8,128)(2,1)}, u32[]{:S(2)}, u32[]{:S(2)}) async-start(bf16[64,8,2048]{2,1,0:T(8,128)(2,1)} %bitcast.14), calls=%async_computation | async-start | bytes 4194304 | tf_op jit(solution)/shard_map/all_to_all | solution.py:277
  68.2 6.2 %copy-start.2 = (bf16[1,512,768]{2,1,0:T(8,128)(2,1)S(1)}, bf16[1,512,768]{2,1,0:T(8,128)(2,1)}, u32[]{:S(2)}) copy-start(bf16[1,512,768]{2,1,0:T(8,128)(2,1)} %refs_7_.1) | copy-start | bytes 2359300
  68.2 104.8 %all-to-all-start.2 = ((bf16[64,8,2048]{2,1,0:T(8,128)(2,1)}), bf16[64,8,2048]{2,1,0:T(8,128)(2,1)}, u32[]{:S(2)}, u32[]{:S(2)}) async-start(bf16[64,8,2048]{2,1,0:T(8,128)(2,1)} %bitcast.13), calls=%async_computation.2 | async-start | bytes 4194304 | tf_op jit(solution)/shard_map/all_to_all | solution.py:277
  74.4 1.1 copy-start.3
  75.6 52.9 %collective-permute-start.1 = (bf16[3,512,768]{2,1,0:T(8,128)(2,1)S(1)}, bf16[3,512,768]{2,1,0:T(8,128)(2,1)S(1)}, u32[]{:S(2)}, u32[]{:S(2)}) collective-permute-start(bf16[3,512,768]{2,1,0:T(8,128)(2,1)S(1)} %constant_dynamic-update-slice_fusion), channel_id=1, source_target_pairs={{0,192},{64,0},{128,64},{192,128},{1,193},{65,1},{129,65},{193,129... | collective-permute-start | bytes 7077896 | tf_op jit(solution)/shard_map/ppermute | solution.py:282
  78.4 53.6 %collective-permute-start = (bf16[3,512,768]{2,1,0:T(8,128)(2,1)S(1)}, bf16[3,512,768]{2,1,0:T(8,128)(2,1)S(1)}, u32[]{:S(2)}, u32[]{:S(2)}) collective-permute-start(bf16[3,512,768]{2,1,0:T(8,128)(2,1)S(1)} %constant_dynamic-update-slice_fusion), channel_id=1, source_target_pairs={{0,64},{64,128},{128,192},{192,0},{1,65},{65,129},{129,193},{193,1... | collective-permute-start | bytes 7077896 | tf_op jit(solution)/shard_map/ppermute | solution.py:282
  128.5 3.7 %copy-start = (bf16[3,512,768]{2,1,0:T(8,128)(2,1)}, bf16[3,512,768]{2,1,0:T(8,128)(2,1)S(1)}, u32[]{:S(2)}) copy-start(bf16[3,512,768]{2,1,0:T(8,128)(2,1)S(1)} %collective-permute-done.1.refs_2_.refs_7_.refs_3_.refs_4_.refs_9_) | copy-start | bytes 7077892
  128.6 27.4 %collective-permute-start.3 = (bf16[3,256,768]{2,1,0:T(8,128)(2,1)S(1)}, bf16[3,256,768]{2,1,0:T(8,128)(2,1)}, u32[]{:S(2)}, u32[]{:S(2)}) collective-permute-start(bf16[3,256,768]{2,1,0:T(8,128)(2,1)S(1)} %slice.25), channel_id=1, source_target_pairs={{0,192},{64,0},{128,64},{192,128},{1,193},{65,1},{129,65},{193,129... | collective-permute-start | bytes 3538952 | tf_op jit(solution)/shard_map/ppermute | solution.py:282
  132.1 1.4 copy-start.1
  132.2 27.3 %collective-permute-start.2 = (bf16[3,256,768]{2,1,0:T(8,128)(2,1)S(1)}, bf16[3,256,768]{2,1,0:T(8,128)(2,1)}, u32[]{:S(2)}, u32[]{:S(2)}) collective-permute-start(bf16[3,256,768]{2,1,0:T(8,128)(2,1)S(1)} %slice.24), channel_id=1, source_target_pairs={{0,64},{64,128},{128,192},{192,0},{1,65},{65,129},{129,193},{193,1... | collective-permute-start | bytes 3538952 | tf_op jit(solution)/shard_map/ppermute | solution.py:282
  173.0 63.9 %all-to-all-start.1 = ((bf16[64,8,2048]{2,1,0:T(8,128)(2,1)}), bf16[64,8,2048]{2,1,0:T(8,128)(2,1)}, u32[]{:S(2)}, u32[]{:S(2)}) async-start(bf16[64,8,2048]{2,1,0:T(8,128)(2,1)} %bitcast.11), calls=%async_computation.1 | async-start | bytes 4194304 | tf_op jit(solution)/shard_map/all_to_all | solution.py:277
  236.9 103.2 %all-to-all-start.3 = ((bf16[64,8,2048]{2,1,0:T(8,128)(2,1)}), bf16[64,8,2048]{2,1,0:T(8,128)(2,1)}, u32[]{:S(2)}, u32[]{:S(2)}) async-start(bf16[64,8,2048]{2,1,0:T(8,128)(2,1)} %bitcast.12), calls=%async_computation.3 | async-start | bytes 4194304 | tf_op jit(solution)/shard_map/all_to_all | solution.py:277
  249.6 36.9 %collective-permute-start.4 = (bf16[512,1536]{1,0:T(8,128)(2,1)}, bf16[512,1536]{1,0:T(8,128)(2,1)}, u32[]{:S(2)}, u32[]{:S(2)}) collective-permute-start(bf16[512,1536]{1,0:T(8,128)(2,1)} %get-tuple-element.40), channel_id=1, source_target_pairs={{0,64},{64,128},{128,192},{192,0},{1,65},{65,129},{129,193},{193,1... | collective-permute-start | bytes 4718600 | tf_op jit(solution)/shard_map/ppermute | solution.py:282
  249.6 39.4 %collective-permute-start.5 = (bf16[512,1536]{1,0:T(8,128)(2,1)}, bf16[512,1536]{1,0:T(8,128)(2,1)}, u32[]{:S(2)}, u32[]{:S(2)}) collective-permute-start(bf16[512,1536]{1,0:T(8,128)(2,1)} %get-tuple-element.41), channel_id=1, source_target_pairs={{0,192},{64,0},{128,64},{192,128},{1,193},{65,1},{129,65},{193,129... | collective-permute-start | bytes 4718600 | tf_op jit(solution)/shard_map/ppermute | solution.py:282
  256.8 32.2 %copy-start.6 = (bf16[256,1536]{1,0:T(8,128)(2,1)S(1)}, bf16[256,1536]{1,0:T(8,128)(2,1)}, u32[]{:S(2)}) copy-start(bf16[256,1536]{1,0:T(8,128)(2,1)} %get-tuple-element.43) | copy-start | bytes 2359300
  256.8 46.5 %collective-permute-start.8 = (bf16[512,768]{1,0:T(8,128)(2,1)}, bf16[512,768]{1,0:T(8,128)(2,1)S(1)}, u32[]{:S(2)}, u32[]{:S(2)}) collective-permute-start(bf16[512,768]{1,0:T(8,128)(2,1)} %get-tuple-element.47), channel_id=1, source_target_pairs={{0,64},{64,128},{128,192},{192,0},{1,65},{65,129},{129,193},{193,1... | collective-permute-start | bytes 2359304 | tf_op jit(solution)/shard_map/ppermute | solution.py:282
  256.8 48.2 %collective-permute-start.9 = (bf16[512,768]{1,0:T(8,128)(2,1)}, bf16[512,768]{1,0:T(8,128)(2,1)S(1)}, u32[]{:S(2)}, u32[]{:S(2)}) collective-permute-start(bf16[512,768]{1,0:T(8,128)(2,1)} %get-tuple-element.48), channel_id=1, source_target_pairs={{0,192},{64,0},{128,64},{192,128},{1,193},{65,1},{129,65},{193,129... | collective-permute-start | bytes 2359304 | tf_op jit(solution)/shard_map/ppermute | solution.py:282
  289.0 15.2 %copy-start.8 = (bf16[256,768]{1,0:T(8,128)(2,1)S(1)}, bf16[256,768]{1,0:T(8,128)(2,1)}, u32[]{:S(2)}) copy-start(bf16[256,768]{1,0:T(8,128)(2,1)} %get-tuple-element.49) | copy-start | bytes 1179652
  289.0 42.9 %collective-permute-start.6 = (bf16[256,1536]{1,0:T(8,128)(2,1)}, bf16[256,1536]{1,0:T(8,128)(2,1)}, u32[]{:S(2)}, u32[]{:S(2)}) collective-permute-start(bf16[256,1536]{1,0:T(8,128)(2,1)} %add_convert_fusion.1), channel_id=1, source_target_pairs={{0,64},{64,128},{128,192},{192,0},{1,65},{65,129},{129,193},{193,1... | collective-permute-start | bytes 2359304 | tf_op jit(solution)/shard_map/ppermute | solution.py:282
  289.0 16.9 %copy-start.7 = (bf16[256,768]{1,0:T(8,128)(2,1)S(1)}, bf16[256,768]{1,0:T(8,128)(2,1)}, u32[]{:S(2)}) copy-start(bf16[256,768]{1,0:T(8,128)(2,1)} %get-tuple-element.50) | copy-start | bytes 1179652
  291.3 40.6 %collective-permute-start.7 = (bf16[256,1536]{1,0:T(8,128)(2,1)}, bf16[256,1536]{1,0:T(8,128)(2,1)}, u32[]{:S(2)}, u32[]{:S(2)}) collective-permute-start(bf16[256,1536]{1,0:T(8,128)(2,1)} %add_convert_fusion), channel_id=1, source_target_pairs={{0,192},{64,0},{128,64},{192,128},{1,193},{65,1},{129,65},{193,129... | collective-permute-start | bytes 2359304 | tf_op jit(solution)/shard_map/ppermute | solution.py:282
  303.3 0.9 copy-start.4
  305.0 23.7 %collective-permute-start.10 = (bf16[256,768]{1,0:T(8,128)(2,1)}, bf16[256,768]{1,0:T(8,128)(2,1)}, u32[]{:S(2)}, u32[]{:S(2)}) collective-permute-start(bf16[256,768]{1,0:T(8,128)(2,1)} %add_convert_fusion.3), channel_id=1, source_target_pairs={{0,64},{64,128},{128,192},{192,0},{1,65},{65,129},{129,193},{193,1... | collective-permute-start | bytes 1179656 | tf_op jit(solution)/shard_map/ppermute | solution.py:282
  305.0 0.9 copy-start.5
  306.8 21.9 %collective-permute-start.11 = (bf16[256,768]{1,0:T(8,128)(2,1)}, bf16[256,768]{1,0:T(8,128)(2,1)}, u32[]{:S(2)}, u32[]{:S(2)}) collective-permute-start(bf16[256,768]{1,0:T(8,128)(2,1)} %add_convert_fusion.2), channel_id=1, source_target_pairs={{0,192},{64,0},{128,64},{192,128},{1,193},{65,1},{129,65},{193,129... | collective-permute-start | bytes 1179656 | tf_op jit(solution)/shard_map/ppermute | solution.py:282
where the time goes:
time: 344 us; the launch traced here: 343 us
  waiting for transfers between devices  211 us (61%)
  Pallas kernels  64.2 us (19%)
  starting transfers between devices  55.2 us (16%)
  other arithmetic  6.38 us (2%)
  local copies, waits for them, and re-layouts  5.54 us (2%)
    ppermute x12, waiting for transfers between devices, shift(): return lax.ppermute(x, 'dp', [(i, (i + by) % 4) for i in range(4)])  128 us
    all_to_all x4, waiting for transfers between devices, move_rows(): lax.all_to_all(buffer, 'expert', split_axis=0, concat_axis=0, tiled=True)  82.7 us
    all_to_all x4, starting transfers between devices, move_rows(): lax.all_to_all(buffer, 'expert', split_axis=0, concat_axis=0, tiled=True)  38.1 us
    ppermute x12, starting transfers between devices, shift(): return lax.ppermute(x, 'dp', [(i, (i + by) % 4) for i in range(4)])  17.1 us
    pallas_call x2, Pallas kernels, by_hidden(): return call(y, rows, *[w for w, _ in weights], *acts)  15.4 us
    pallas_call x2, Pallas kernels, spread(): return call(y, *acts, *[w for w, _ in flat])  13.2 us
    pallas_call x2, Pallas kernels, partials(): whole(functools.partial(partial_kernel, len(acts)), [full, full, full, ha...  11.2 us
    pallas_call x2, Pallas kernels, ring_sum(): whole(sum_kernel, [shape_of((1, size, wide // parts), F32)] * parts, 5, n...  7.92 us
  transfers between devices with their start and end apart: 16, of which 8 were waited for; matrix products, arithmetic and copies ran while one was open for 2% of the time, Pallas kernels for 17%

commit v1 on v0

--- a/solution.py
+++ b/solution.py
@@ -21,13 +21,13 @@
     return jax.ShapeDtypeStruct(shape, dtype)
 
 
-def whole(kernel, outs, n_in, flops=0, nbytes=0, smem=()):
+def whole(kernel, outs, n_in, flops=0, nbytes=0, smem=(), limit=LIMIT):
     call = pl.pallas_call(
         kernel,
         out_shape=outs,
         in_specs=[SMEM if i in smem else VMEM for i in range(n_in)],
         out_specs=[VMEM for _ in outs],
-        compiler_params=pltpu.CompilerParams(vmem_limit_bytes=LIMIT),
+        compiler_params=pltpu.CompilerParams(vmem_limit_bytes=limit),
         cost_estimate=pl.CostEstimate(flops=flops, bytes_accessed=nbytes, transcendentals=0),
     )
     return call
@@ -301,7 +301,11 @@
     dn_b = (dn_b.astype(F32) + got_dn[:half].astype(F32)).astype(BF)
     below, above = shift(up_a, 1), shift(dn_b, -1)
     return whole(
-        sum_kernel, [shape_of((1, size, wide // parts), F32)] * parts, 5, nbytes=12 * size * wide
+        sum_kernel,
+        [shape_of((1, size, wide // parts), F32)] * parts,
+        5,
+        nbytes=12 * size * wide,
+        limit=24 * 2**20,
     )(own, got_up, got_dn, below, above)
 
 
@@ -356,11 +360,11 @@
     )
     grad_in = spread(y, [grad_gate, grad_up], [w_gate, w_up])
     grad_back = move_rows(grad_in, members)
-    output = whole(output_kernel, [shape_of((count, width), BF)], 2, nbytes=3 * 2**20)(
+    output = whole(output_kernel, [shape_of((count, width), BF)], 2, nbytes=3 * 2**20, limit=16 * 2**20)(
         pieces, returned
     )[0]
     token_grad = whole(
-        token_grad_kernel, [shape_of((count, width), BF)], 2, nbytes=3 * 2**20
+        token_grad_kernel, [shape_of((count, width), BF)], 2, nbytes=3 * 2**20, limit=16 * 2**20
     )(pick, grad_back)[0]
 
     down_grad = ring_sum(1, *partials(y, grad_rows, [hid], size))[0]

time: 344 us -> 347 us (level)
    unnamed x20 -> x32, local copies, waits for them, and re-layouts: 5.34 us -> 8.74 us
  transfers between devices with their start and end apart: 16 -> 16, of which waited for: 8 -> 8; matrix products, arithmetic and copies ran while one was open for 2% -> 2% of each run, Pallas kernels for 17% -> 16%
where the time goes in v1:
time: 347 us; the launch traced here: 345 us
  waiting for transfers between devices  211 us (61%)
  Pallas kernels  62.9 us (18%)
  starting transfers between devices  55.2 us (16%)
  local copies, waits for them, and re-layouts  8.95 us (3%)
  other arithmetic  6.42 us (2%)
    ppermute x12, waiting for transfers between devices, shift(): return lax.ppermute(x, 'dp', [(i, (i + by) % 4) for i in range(4)])  128 us
    all_to_all x4, waiting for transfers between devices, move_rows(): lax.all_to_all(buffer, 'expert', split_axis=0, concat_axis=0, tiled=True)  82.8 us
    all_to_all x4, starting transfers between devices, move_rows(): lax.all_to_all(buffer, 'expert', split_axis=0, concat_axis=0, tiled=True)  38.1 us
    ppermute x12, starting transfers between devices, shift(): return lax.ppermute(x, 'dp', [(i, (i + by) % 4) for i in range(4)])  17 us
    pallas_call x2, Pallas kernels, by_hidden(): return call(y, rows, *[w for w, _ in weights], *acts)  15.4 us
    pallas_call x2, Pallas kernels, spread(): return call(y, *acts, *[w for w, _ in flat])  13.2 us
    pallas_call x2, Pallas kernels, partials(): whole(functools.partial(partial_kernel, len(acts)), [full, full, full, ha...  11.2 us
    unnamed x32, local copies, waits for them, and re-layouts  8.74 us
  transfers between devices with their start and end apart: 16, of which 8 were waited for; matrix products, arithmetic and copies ran while one was open for 2% of the time, Pallas kernels for 16%

profile of v1, /device:TPU:1, one launch (start us, length us, event | category | flops | bytes accessed | tf_op | source)
XLA Modules:
  0.0 345.4 jit_solution(6954465776765825197)
XLA Ops:
  0.6 3.3 shard_map.128
  4.0 13.2 %all-to-all-start = ((bf16[64,8,2048]{2,1,0:T(8,128)(2,1)}), bf16[64,8,2048]{2,1,0:T(8,128)(2,1)}, u32[]{:S(2)}, u32[]{:S(2)}) async-start(bf16[64,8,2048]{2,1,0:T(8,128)(2,1)} %bitcast.14), calls=%async_computation | async-start | bytes 4194304 | tf_op jit(solution)/shard_map/all_to_all | solution.py:277
  17.1 3.2 shard_map.129
  20.3 1.2 constant_dynamic-update-slice_fusion.2
  21.5 46.7 %all-to-all-done = bf16[64,8,2048]{2,1,0:T(8,128)(2,1)} async-done(((bf16[64,8,2048]{2,1,0:T(8,128)(2,1)}), bf16[64,8,2048]{2,1,0:T(8,128)(2,1)}, u32[]{:S(2)}, u32[]{:S(2)}) %all-to-all-start) | async-done | bytes 2097184 | tf_op jit(solution)/shard_map/all_to_all | solution.py:277
  68.3 6.2 %all-to-all-start.2 = ((bf16[64,8,2048]{2,1,0:T(8,128)(2,1)}), bf16[64,8,2048]{2,1,0:T(8,128)(2,1)}, u32[]{:S(2)}, u32[]{:S(2)}) async-start(bf16[64,8,2048]{2,1,0:T(8,128)(2,1)} %bitcast.13), calls=%async_computation.2 | async-start | bytes 4194304 | tf_op jit(solution)/shard_map/all_to_all | solution.py:277
  74.4 0.0 copy-start.11
  74.5 0.1 constant_dynamic-update-slice_fusion.1
  74.5 1.1 copy-done.11
  75.6 0.1 constant_dynamic-update-slice_fusion
  75.6 2.8 collective-permute-start.1
  78.4 0.0 collective-permute-start
  78.4 50.1 %collective-permute-done.1.refs_2_.refs_7_.refs_3_.refs_4_.refs_9_ = bf16[3,512,768]{2,1,0:T(8,128)(2,1)S(1)} collective-permute-done((bf16[3,512,768]{2,1,0:T(8,128)(2,1)S(1)}, bf16[3,512,768]{2,1,0:T(8,128)(2,1)S(1)}, u32[]{:S(2)}, u32[]{:S(2)}) %collective-permute-start.1) | collective-permute-done | bytes 2359328 | tf_op jit(solution)/shard_map/ppermute | solution.py:282
  128.5 0.1 slice.25
  128.6 3.5 %collective-permute-start.3 = (bf16[3,256,768]{2,1,0:T(8,128)(2,1)S(1)}, bf16[3,256,768]{2,1,0:T(8,128)(2,1)}, u32[]{:S(2)}, u32[]{:S(2)}) collective-permute-start(bf16[3,256,768]{2,1,0:T(8,128)(2,1)S(1)} %slice.25), channel_id=1, source_target_pairs={{0,192},{64,0},{128,64},{192,128},{1,193},{65,1},{129,65},{193,129... | collective-permute-start | bytes 3538952 | tf_op jit(solution)/shard_map/ppermute | solution.py:282
  132.1 0.0 collective-permute-done.refs_1_.refs_6_.refs_2_.refs_3_.refs_8_
  132.1 0.1 slice.24
  132.2 0.1 collective-permute-start.2
  132.3 1.2 copy-done.9
  133.5 22.5 %collective-permute-done.3.refs_4_.refs_9_.refs_5_.refs_6_.refs_11_ = bf16[3,256,768]{2,1,0:T(8,128)(2,1)} collective-permute-done((bf16[3,256,768]{2,1,0:T(8,128)(2,1)S(1)}, bf16[3,256,768]{2,1,0:T(8,128)(2,1)}, u32[]{:S(2)}, u32[]{:S(2)}) %collective-permute-start.3) | collective-permute-done | bytes 1179680 | tf_op jit(solution)/shard_map/ppermute | solution.py:282
  156.0 3.4 collective-permute-done.2.refs_3_.refs_8_.refs_4_.refs_5_.refs_10_
  159.4 8.4 %shard_map.132 = (f32[512,768]{1,0:T(8,128)}, f32[512,768]{1,0:T(8,128)}, bf16[512,768]{1,0:T(8,128)(2,1)}) custom-call(s32[1]{0:T(128)} %bitcast.2.y_ref, bf16[512,2048]{1,0:T(8,128)(2,1)} %bitcast.4.rows_ref, bf16[1,512,768]{2,1,0:T(8,128)(2,1)} %refs_2_.1, bf16[3,512,768]{2,1,0:T(8,128)(2,1)} %copy-done.9, bf16[3,512,768]{2,1,0:T(8,128)(2,1)} %copy-done.8, ...), custom_call_target="tpu_custom_call" | custom-call | flops 3221225472 | bytes 11534336 | tf_op jit(solution)/shard_map/pallas_call | solution.py:170
  167.9 5.2 %shard_map.133 = bf16[512,2048]{1,0:T(8,128)(2,1)} custom-call(s32[1]{0:T(128)} %bitcast.2.y_ref, bf16[512,768]{1,0:T(8,128)(2,1)} %get-tuple-element.32.refs_0_, bf16[1,512,768]{2,1,0:T(8,128)(2,1)} %refs_0_.3, bf16[3,512,768]{2,1,0:T(8,128)(2,1)} %copy-done.9, bf16[3,512,768]{2,1,0:T(8,128)(2,1)} %copy-done.8, ...), custom_call_target="tpu_custom_call" | custom-call | flops 1610612736 | bytes 5242880 | tf_op jit(solution)/shard_map/pallas_call | solution.py:209
  173.1 0.0 all-to-all-done.2
  173.1 12.8 %all-to-all-start.1 = ((bf16[64,8,2048]{2,1,0:T(8,128)(2,1)}), bf16[64,8,2048]{2,1,0:T(8,128)(2,1)}, u32[]{:S(2)}, u32[]{:S(2)}) async-start(bf16[64,8,2048]{2,1,0:T(8,128)(2,1)} %bitcast.11), calls=%async_computation.1 | async-start | bytes 4194304 | tf_op jit(solution)/shard_map/all_to_all | solution.py:277
  185.9 7.0 %shard_map.135 = (bf16[512,768]{1,0:T(8,128)(2,1)}, bf16[512,768]{1,0:T(8,128)(2,1)}) custom-call(s32[1]{0:T(128)} %bitcast.2.y_ref, bf16[512,2048]{1,0:T(8,128)(2,1)} %bitcast.8.rows_ref, bf16[1,512,768]{2,1,0:T(8,128)(2,1)} %refs_0_.3, bf16[3,512,768]{2,1,0:T(8,128)(2,1)} %copy-done.9, bf16[3,512,768]{2,1,0:T(8,128)(2,1)} %copy-done.8, ...), custom_call_target="tpu_custom_call" | custom-call | flops 1610612736 | bytes 8388608 | tf_op jit(solution)/shard_map/pallas_call | solution.py:170
  192.8 8.1 %shard_map.136 = bf16[512,2048]{1,0:T(8,128)(2,1)} custom-call(s32[1]{0:T(128)} %bitcast.2.y_ref, bf16[512,768]{1,0:T(8,128)(2,1)} %get-tuple-element.37.refs_0_, bf16[512,768]{1,0:T(8,128)(2,1)} %get-tuple-element.38.refs_1_, bf16[1,512,768]{2,1,0:T(8,128)(2,1)} %refs_2_.1, bf16[3,512,768]{2,1,0:T(8,128)(2,1)} %copy-done.9, bf16[3,512,768]{2,1,0:T(8,128)(2,1)} %copy-done.8, ...), custom_call_target="tpu_custom_call" | custom-call | flops 3221225472 | bytes 8388608 | tf_op jit(solution)/shard_map/pallas_call | solution.py:209
  200.9 36.1 %all-to-all-done.1 = bf16[64,8,2048]{2,1,0:T(8,128)(2,1)} async-done(((bf16[64,8,2048]{2,1,0:T(8,128)(2,1)}), bf16[64,8,2048]{2,1,0:T(8,128)(2,1)}, u32[]{:S(2)}, u32[]{:S(2)}) %all-to-all-start.1) | async-done | bytes 2097184 | tf_op jit(solution)/shard_map/all_to_all | solution.py:277
  237.0 6.0 %all-to-all-start.3 = ((bf16[64,8,2048]{2,1,0:T(8,128)(2,1)}), bf16[64,8,2048]{2,1,0:T(8,128)(2,1)}, u32[]{:S(2)}, u32[]{:S(2)}) async-start(bf16[64,8,2048]{2,1,0:T(8,128)(2,1)} %bitcast.12), calls=%async_computation.3 | async-start | bytes 4194304 | tf_op jit(solution)/shard_map/all_to_all | solution.py:277
  243.0 6.6 %shard_map.138 = (bf16[512,1536]{1,0:T(8,128)(2,1)}, bf16[512,1536]{1,0:T(8,128)(2,1)}, bf16[512,1536]{1,0:T(8,128)(2,1)}, bf16[256,1536]{1,0:T(8,128)(2,1)}, bf16[256,1536]{1,0:T(8,128)(2,1)}) custom-call(s32[1]{0:T(128)} %bitcast.2.y_ref, bf16[512,2048]{1,0:T(8,128)(2,1)} %bitcast.4.rows_ref, bf16[512,768]{1,0:T(8,128)(2,1)} %get-tuple-element.37.refs_0_, ...), custom_call_target="tpu_custom_call" | custom-call | flops 3221225472 | bytes 8388608 | tf_op jit(solution)/shard_map/pallas_call | solution.py:233
  249.7 0.0 collective-permute-start.4
  249.7 2.7 collective-permute-start.5
  252.3 4.5 %shard_map.140 = (bf16[512,768]{1,0:T(8,128)(2,1)}, bf16[512,768]{1,0:T(8,128)(2,1)}, bf16[512,768]{1,0:T(8,128)(2,1)}, bf16[256,768]{1,0:T(8,128)(2,1)}, bf16[256,768]{1,0:T(8,128)(2,1)}) custom-call(s32[1]{0:T(128)} %bitcast.2.y_ref, bf16[512,2048]{1,0:T(8,128)(2,1)} %bitcast.8.rows_ref, bf16[512,768]{1,0:T(8,128)(2,1)} %get-tuple-element.32.refs_0_), custom_call_target="tpu_custom_call" | custom-call | flops 1610612736 | bytes 5242880 | tf_op jit(solution)/shard_map/pallas_call | solution.py:233
  256.9 0.0 collective-permute-start.8
  256.9 2.7 collective-permute-start.9
  259.5 27.1 %collective-permute-done.4.up_ref = bf16[512,1536]{1,0:T(8,128)(2,1)} collective-permute-done((bf16[512,1536]{1,0:T(8,128)(2,1)}, bf16[512,1536]{1,0:T(8,128)(2,1)}, u32[]{:S(2)}, u32[]{:S(2)}) %collective-permute-start.4) | collective-permute-done | bytes 1572896 | tf_op jit(solution)/shard_map/ppermute | solution.py:282
  286.6 2.4 add_convert_fusion.1
  289.1 0.0 collective-permute-start.6
  289.1 0.0 collective-permute-done.5.dn_ref
  289.1 0.0 copy-start.13
  289.1 2.3 add_convert_fusion
  291.4 2.6 collective-permute-start.7
  294.0 9.4 %collective-permute-done.8.up_ref = bf16[512,768]{1,0:T(8,128)(2,1)S(1)} collective-permute-done((bf16[512,768]{1,0:T(8,128)(2,1)}, bf16[512,768]{1,0:T(8,128)(2,1)S(1)}, u32[]{:S(2)}, u32[]{:S(2)}) %collective-permute-start.8) | collective-permute-done | bytes 786464 | tf_op jit(solution)/shard_map/ppermute | solution.py:282
  303.4 0.9 add_convert_fusion.3
  304.2 0.9 copy-done
  305.1 0.0 collective-permute-start.10
  305.1 0.0 collective-permute-done.9.dn_ref
  305.1 0.8 add_convert_fusion.2
  306.0 0.9 copy-done.2
  306.8 2.7 collective-permute-start.11
  309.5 1.7 shard_map.130
  311.2 1.8 shard_map.131.pieces_ref
  312.9 15.8 %collective-permute-done.10.below_ref = bf16[256,768]{1,0:T(8,128)(2,1)} collective-permute-done((bf16[256,768]{1,0:T(8,128)(2,1)}, bf16[256,768]{1,0:T(8,128)(2,1)}, u32[]{:S(2)}, u32[]{:S(2)}) %collective-permute-start.10) | collective-permute-done | bytes 393248 | tf_op jit(solution)/shard_map/ppermute | solution.py:282
  328.7 0.0 collective-permute-done.11.above_ref
  328.7 1.1 copy-done.1
  329.9 1.1 copy-done.3
  331.0 1.1 copy-done.6
  332.1 2.6 shard_map.141
  334.8 0.0 collective-permute-done.6.below_ref
  334.8 0.0 copy-start.5
  334.8 4.3 %shard_map.139 = (f32[1,512,768]{2,1,0:T(8,128)}, f32[1,512,768]{2,1,0:T(8,128)}) custom-call(bf16[512,1536]{1,0:T(8,128)(2,1)S(1)} %copy-done.4, bf16[512,1536]{1,0:T(8,128)(2,1)} %collective-permute-done.4.up_ref, bf16[512,1536]{1,0:T(8,128)(2,1)} %collective-permute-done.5.dn_ref, bf16[256,1536]{1,0:T(8,128)(2,1)} %collective-permute-done.6.below_ref, ...), custom_call_target="tpu_custom_call" | custom-call | bytes 9437184 | tf_op jit(solution)/shard_map/pallas_call | solution.py:303
  339.1 3.4 shard_map.134
  342.5 0.0 all-to-all-done.3
  342.5 2.8 shard_map.137
  (21 shorter events, 0.0 us)
Async XLA Ops:
  4.0 64.3 %all-to-all-start = ((bf16[64,8,2048]{2,1,0:T(8,128)(2,1)}), bf16[64,8,2048]{2,1,0:T(8,128)(2,1)}, u32[]{:S(2)}, u32[]{:S(2)}) async-start(bf16[64,8,2048]{2,1,0:T(8,128)(2,1)} %bitcast.14), calls=%async_computation | async-start | bytes 4194304 | tf_op jit(solution)/shard_map/all_to_all | solution.py:277
  68.3 6.2 %copy-start.10 = (bf16[1,512,768]{2,1,0:T(8,128)(2,1)S(1)}, bf16[1,512,768]{2,1,0:T(8,128)(2,1)}, u32[]{:S(2)}) copy-start(bf16[1,512,768]{2,1,0:T(8,128)(2,1)} %refs_7_.1) | copy-start | bytes 2359300
  68.3 104.8 %all-to-all-start.2 = ((bf16[64,8,2048]{2,1,0:T(8,128)(2,1)}), bf16[64,8,2048]{2,1,0:T(8,128)(2,1)}, u32[]{:S(2)}, u32[]{:S(2)}) async-start(bf16[64,8,2048]{2,1,0:T(8,128)(2,1)} %bitcast.13), calls=%async_computation.2 | async-start | bytes 4194304 | tf_op jit(solution)/shard_map/all_to_all | solution.py:277
  74.4 1.1 copy-start.11
  75.6 52.9 %collective-permute-start.1 = (bf16[3,512,768]{2,1,0:T(8,128)(2,1)S(1)}, bf16[3,512,768]{2,1,0:T(8,128)(2,1)S(1)}, u32[]{:S(2)}, u32[]{:S(2)}) collective-permute-start(bf16[3,512,768]{2,1,0:T(8,128)(2,1)S(1)} %constant_dynamic-update-slice_fusion), channel_id=1, source_target_pairs={{0,192},{64,0},{128,64},{192,128},{1,193},{65,1},{129,65},{193,129... | collective-permute-start | bytes 7077896 | tf_op jit(solution)/shard_map/ppermute | solution.py:282
  78.4 53.6 %collective-permute-start = (bf16[3,512,768]{2,1,0:T(8,128)(2,1)S(1)}, bf16[3,512,768]{2,1,0:T(8,128)(2,1)S(1)}, u32[]{:S(2)}, u32[]{:S(2)}) collective-permute-start(bf16[3,512,768]{2,1,0:T(8,128)(2,1)S(1)} %constant_dynamic-update-slice_fusion), channel_id=1, source_target_pairs={{0,64},{64,128},{128,192},{192,0},{1,65},{65,129},{129,193},{193,1... | collective-permute-start | bytes 7077896 | tf_op jit(solution)/shard_map/ppermute | solution.py:282
  128.5 3.7 %copy-start.8 = (bf16[3,512,768]{2,1,0:T(8,128)(2,1)}, bf16[3,512,768]{2,1,0:T(8,128)(2,1)S(1)}, u32[]{:S(2)}) copy-start(bf16[3,512,768]{2,1,0:T(8,128)(2,1)S(1)} %collective-permute-done.1.refs_2_.refs_7_.refs_3_.refs_4_.refs_9_) | copy-start | bytes 7077892
  128.6 27.4 %collective-permute-start.3 = (bf16[3,256,768]{2,1,0:T(8,128)(2,1)S(1)}, bf16[3,256,768]{2,1,0:T(8,128)(2,1)}, u32[]{:S(2)}, u32[]{:S(2)}) collective-permute-start(bf16[3,256,768]{2,1,0:T(8,128)(2,1)S(1)} %slice.25), channel_id=1, source_target_pairs={{0,192},{64,0},{128,64},{192,128},{1,193},{65,1},{129,65},{193,129... | collective-permute-start | bytes 3538952 | tf_op jit(solution)/shard_map/ppermute | solution.py:282
  132.1 1.4 copy-start.9
  132.2 27.3 %collective-permute-start.2 = (bf16[3,256,768]{2,1,0:T(8,128)(2,1)S(1)}, bf16[3,256,768]{2,1,0:T(8,128)(2,1)}, u32[]{:S(2)}, u32[]{:S(2)}) collective-permute-start(bf16[3,256,768]{2,1,0:T(8,128)(2,1)S(1)} %slice.24), channel_id=1, source_target_pairs={{0,64},{64,128},{128,192},{192,0},{1,65},{65,129},{129,193},{193,1... | collective-permute-start | bytes 3538952 | tf_op jit(solution)/shard_map/ppermute | solution.py:282
  173.1 63.9 %all-to-all-start.1 = ((bf16[64,8,2048]{2,1,0:T(8,128)(2,1)}), bf16[64,8,2048]{2,1,0:T(8,128)(2,1)}, u32[]{:S(2)}, u32[]{:S(2)}) async-start(bf16[64,8,2048]{2,1,0:T(8,128)(2,1)} %bitcast.11), calls=%async_computation.1 | async-start | bytes 4194304 | tf_op jit(solution)/shard_map/all_to_all | solution.py:277
  237.0 105.5 %all-to-all-start.3 = ((bf16[64,8,2048]{2,1,0:T(8,128)(2,1)}), bf16[64,8,2048]{2,1,0:T(8,128)(2,1)}, u32[]{:S(2)}, u32[]{:S(2)}) async-start(bf16[64,8,2048]{2,1,0:T(8,128)(2,1)} %bitcast.12), calls=%async_computation.3 | async-start | bytes 4194304 | tf_op jit(solution)/shard_map/all_to_all | solution.py:277
  249.7 36.9 %collective-permute-start.4 = (bf16[512,1536]{1,0:T(8,128)(2,1)}, bf16[512,1536]{1,0:T(8,128)(2,1)}, u32[]{:S(2)}, u32[]{:S(2)}) collective-permute-start(bf16[512,1536]{1,0:T(8,128)(2,1)} %get-tuple-element.40), channel_id=1, source_target_pairs={{0,64},{64,128},{128,192},{192,0},{1,65},{65,129},{129,193},{193,1... | collective-permute-start | bytes 4718600 | tf_op jit(solution)/shard_map/ppermute | solution.py:282
  249.7 39.4 %collective-permute-start.5 = (bf16[512,1536]{1,0:T(8,128)(2,1)}, bf16[512,1536]{1,0:T(8,128)(2,1)}, u32[]{:S(2)}, u32[]{:S(2)}) collective-permute-start(bf16[512,1536]{1,0:T(8,128)(2,1)} %get-tuple-element.41), channel_id=1, source_target_pairs={{0,192},{64,0},{128,64},{192,128},{1,193},{65,1},{129,65},{193,129... | collective-permute-start | bytes 4718600 | tf_op jit(solution)/shard_map/ppermute | solution.py:282
  256.9 32.2 %copy-start.12 = (bf16[256,1536]{1,0:T(8,128)(2,1)S(1)}, bf16[256,1536]{1,0:T(8,128)(2,1)}, u32[]{:S(2)}) copy-start(bf16[256,1536]{1,0:T(8,128)(2,1)} %get-tuple-element.43) | copy-start | bytes 2359300
  256.9 46.5 %collective-permute-start.8 = (bf16[512,768]{1,0:T(8,128)(2,1)}, bf16[512,768]{1,0:T(8,128)(2,1)S(1)}, u32[]{:S(2)}, u32[]{:S(2)}) collective-permute-start(bf16[512,768]{1,0:T(8,128)(2,1)} %get-tuple-element.47), channel_id=1, source_target_pairs={{0,64},{64,128},{128,192},{192,0},{1,65},{65,129},{129,193},{193,1... | collective-permute-start | bytes 2359304 | tf_op jit(solution)/shard_map/ppermute | solution.py:282
  256.9 48.2 %collective-permute-start.9 = (bf16[512,768]{1,0:T(8,128)(2,1)}, bf16[512,768]{1,0:T(8,128)(2,1)S(1)}, u32[]{:S(2)}, u32[]{:S(2)}) collective-permute-start(bf16[512,768]{1,0:T(8,128)(2,1)} %get-tuple-element.48), channel_id=1, source_target_pairs={{0,192},{64,0},{128,64},{192,128},{1,193},{65,1},{129,65},{193,129... | collective-permute-start | bytes 2359304 | tf_op jit(solution)/shard_map/ppermute | solution.py:282
  289.1 14.3 %copy-start.14 = (bf16[256,768]{1,0:T(8,128)(2,1)S(1)}, bf16[256,768]{1,0:T(8,128)(2,1)}, u32[]{:S(2)}) copy-start(bf16[256,768]{1,0:T(8,128)(2,1)} %get-tuple-element.49) | copy-start | bytes 1179652
  289.1 45.7 %collective-permute-start.6 = (bf16[256,1536]{1,0:T(8,128)(2,1)}, bf16[256,1536]{1,0:T(8,128)(2,1)}, u32[]{:S(2)}, u32[]{:S(2)}) collective-permute-start(bf16[256,1536]{1,0:T(8,128)(2,1)} %add_convert_fusion.1), channel_id=1, source_target_pairs={{0,64},{64,128},{128,192},{192,0},{1,65},{65,129},{129,193},{193,1... | collective-permute-start | bytes 2359304 | tf_op jit(solution)/shard_map/ppermute | solution.py:282
  289.1 16.0 %copy-start.13 = (bf16[256,768]{1,0:T(8,128)(2,1)S(1)}, bf16[256,768]{1,0:T(8,128)(2,1)}, u32[]{:S(2)}) copy-start(bf16[256,768]{1,0:T(8,128)(2,1)} %get-tuple-element.50) | copy-start | bytes 1179652
  291.4 43.4 %collective-permute-start.7 = (bf16[256,1536]{1,0:T(8,128)(2,1)}, bf16[256,1536]{1,0:T(8,128)(2,1)}, u32[]{:S(2)}, u32[]{:S(2)}) collective-permute-start(bf16[256,1536]{1,0:T(8,128)(2,1)} %add_convert_fusion), channel_id=1, source_target_pairs={{0,192},{64,0},{128,64},{192,128},{1,193},{65,1},{129,65},{193,129... | collective-permute-start | bytes 2359304 | tf_op jit(solution)/shard_map/ppermute | solution.py:282
  304.2 0.9 copy-start
  305.1 23.6 %collective-permute-start.10 = (bf16[256,768]{1,0:T(8,128)(2,1)}, bf16[256,768]{1,0:T(8,128)(2,1)}, u32[]{:S(2)}, u32[]{:S(2)}) collective-permute-start(bf16[256,768]{1,0:T(8,128)(2,1)} %add_convert_fusion.3), channel_id=1, source_target_pairs={{0,64},{64,128},{128,192},{192,0},{1,65},{65,129},{129,193},{193,1... | collective-permute-start | bytes 1179656 | tf_op jit(solution)/shard_map/ppermute | solution.py:282
  306.0 0.9 copy-start.2
  306.8 21.9 %collective-permute-start.11 = (bf16[256,768]{1,0:T(8,128)(2,1)}, bf16[256,768]{1,0:T(8,128)(2,1)}, u32[]{:S(2)}, u32[]{:S(2)}) collective-permute-start(bf16[256,768]{1,0:T(8,128)(2,1)} %add_convert_fusion.2), channel_id=1, source_target_pairs={{0,192},{64,0},{128,64},{192,128},{1,193},{65,1},{129,65},{193,129... | collective-permute-start | bytes 1179656 | tf_op jit(solution)/shard_map/ppermute | solution.py:282
  328.7 1.1 copy-start.1
  329.9 1.1 copy-start.3
  331.0 1.1 copy-start.6
  332.1 2.6 copy-start.4
  334.8 4.3 %copy-start.5 = (bf16[3,128,512]{2,1,0:T(8,128)(2,1)S(1)}, bf16[3,128,512]{2,1,0:T(8,128)(2,1)}, u32[]{:S(2)}) copy-start(bf16[3,128,512]{2,1,0:T(8,128)(2,1)} %shard_map.131.pieces_ref) | copy-start | bytes 1179652
  339.1 3.4 copy-start.7

commit v2 on v1

v2 whole, which is shorter than its diff:
```python
import functools

import jax
import jax.numpy as jnp
from jax import lax
from jax.experimental import pallas as pl
from jax.experimental.pallas import tpu as pltpu
from jax.sharding import PartitionSpec as P


BF = jnp.bfloat16
F32 = jnp.float32
FIRST = (((0,), (0,)), ((), ()))
LAST = (((1,), (1,)), ((), ()))
VMEM = pl.BlockSpec(memory_space=pltpu.VMEM)
SMEM = pl.BlockSpec(memory_space=pltpu.SMEM)
LIMIT = 67_043_328


def shape_of(shape, dtype):
    return jax.ShapeDtypeStruct(shape, dtype)


def whole(kernel, outs, n_in, flops=0, nbytes=0, smem=(), limit=LIMIT):
    call = pl.pallas_call(
        kernel,
        out_shape=outs,
        in_specs=[SMEM if i in smem else VMEM for i in range(n_in)],
        out_specs=[VMEM for _ in outs],
        compiler_params=pltpu.CompilerParams(vmem_limit_bytes=limit),
        cost_estimate=pl.CostEstimate(flops=flops, bytes_accessed=nbytes, transcendentals=0),
    )
    return call


def chosen(place, slots):
    spots = lax.broadcasted_iota(jnp.int32, (slots, place.shape[1]), 0)
    return [place[k : k + 1, :] == spots for k in range(place.shape[0])]


def added(terms):
    total = terms[0]
    for term in terms[1:]:
        total = total + term
    return total


def send_kernel(
    members,
    capacity,
    bucket_ref,
    table_ref,
    ids_ref,
    level_ref,
    tokens_ref,
    grad_ref,
    rows_ref,
    place_ref,
    gate_ref,
):
    top, count = ids_ref.shape
    width = tokens_ref.shape[1]
    names = lax.broadcasted_iota(jnp.int32, (members, count), 0)
    before = (
        lax.broadcasted_iota(jnp.int32, (count, count), 0)
        < lax.broadcasted_iota(jnp.int32, (count, count), 1)
    ).astype(BF)
    ahead = jnp.zeros((members, 1), F32)
    places = []
    for k in range(top):
        ids = ids_ref[k : k + 1, :]
        hot = (ids == names).astype(F32)
        earlier = jnp.dot(hot.astype(BF), before, preferred_element_type=F32) + ahead
        rank = jnp.sum(hot * earlier, axis=0, keepdims=True).astype(jnp.int32)
        ahead = ahead + jnp.sum(hot, axis=1, keepdims=True)
        places.append(ids * capacity + rank)
        place_ref[k : k + 1, :] = places[-1]
    trajs = bucket_ref.shape[0]
    level = level_ref[...]
    traj = lax.broadcasted_iota(jnp.int32, (top, count), 1) // (count // trajs)
    gate = jnp.zeros((top, count), F32)
    for at in range(table_ref.shape[1]):
        entry = jnp.zeros((top, count), F32)
        for j in range(trajs):
            entry = jnp.where(traj == j, table_ref[bucket_ref[j], at], entry)
        gate = jnp.where(level == at, entry, gate)
    gate_ref[...] = gate
    spots = lax.broadcasted_iota(jnp.int32, (members * capacity, count), 0)
    hots = [place == spots for place in places]
    pick = added([hot.astype(F32) for hot in hots]).astype(BF)
    rows_ref[:, :width] = jnp.dot(pick, tokens_ref[...], preferred_element_type=F32).astype(BF)
    gated = added([jnp.where(hot, gate[k : k + 1, :], 0.0) for k, hot in enumerate(hots)])
    slot_gate = jnp.sum(gated, axis=1, keepdims=True)
    grads = jnp.dot(pick, grad_ref[...], preferred_element_type=F32)
    rows_ref[:, width:] = (grads * slot_gate).astype(BF)


def pick_kernel(place_ref, gate_ref, pick_ref, gated_ref):
    hots = chosen(place_ref[...], pick_ref.shape[1])
    pick_ref[...] = added([hot.astype(F32) for hot in hots]).T.astype(BF)
    gate = gate_ref[...]
    gated_ref[...] = added(
        [jnp.where(hot, gate[k : k + 1, :], 0.0) for k, hot in enumerate(hots)]
    ).T


def split_kernel(gated_ref, pieces_ref):
    rest = gated_ref[...]
    for i in range(pieces_ref.shape[0]):
        piece = rest.astype(BF)
        pieces_ref[i] = piece
        rest = rest - piece.astype(F32)


def columns(offset, size):
    return pl.ds(pl.multiple_of(offset, 128), size)


def offsets(y, n, size):
    at = lambda j: lax.rem(y + j, n) * size
    half = size // 2
    return [(at(0), size), (at(3), size), (at(1), size), (at(2), half), (at(2) + half, half)]


def middle_kernel(
    tile,
    y_ref,
    rows_hbm,
    gate_w,
    up_w,
    down_w,
    below,
    above,
    far_a,
    far_b,
    back_hbm,
    hid_hbm,
    gg_hbm,
    gu_hbm,
    rows,
    w_gate,
    w_up,
    w_down,
    back,
    hid,
    gg,
    gu,
    row_sem,
    weight_sem,
    act_sem,
    back_sem,
):
    hidden = hid.shape[1]
    width = rows.shape[1] // 2
    spots = offsets(y_ref[0], 4, width // 4)

    def fetch_rows(part):
        at = slice(part * width, (part + 1) * width)
        copy = pltpu.make_async_copy(rows_hbm.at[:, at], rows.at[:, at], row_sem.at[part])
        copy.start()
        return [copy]

    def fetch_weight(i, shard, held):
        sources = [shard.at[0]] + [ref.at[i] for ref in (below, above, far_a, far_b)]
        copies = [
            pltpu.make_async_copy(
                source, held.at[pl.ds(pl.multiple_of(off, 256), size), :], weight_sem.at[i, j]
            )
            for j, (source, (off, size)) in enumerate(zip(sources, spots))
        ]
        for copy in copies:
            copy.start()
        return copies

    waits = [
        fetch_rows(0) + fetch_weight(0, gate_w, w_gate),
        fetch_weight(1, up_w, w_up),
        fetch_rows(1) + fetch_weight(2, down_w, w_down),
    ]
    tiles = [slice(at, at + tile) for at in range(0, hidden, tile)]

    def into(i, base, held, at):
        if at.start == 0:
            for copy in waits[i]:
                copy.wait()
        return jnp.dot(rows[:, base : base + width], held[:, at], preferred_element_type=F32)

    for at in tiles:
        gate_act = into(0, 0, w_gate, at)
        up_act = into(1, 0, w_up, at)
        grad = into(2, width, w_down, at)
        s = jax.nn.sigmoid(gate_act)
        swish = gate_act * s
        hid[:, at] = (swish * up_act).astype(BF)
        gg[:, at] = (grad * up_act * s * (1.0 + gate_act * (1.0 - s))).astype(BF)
        gu[:, at] = (grad * swish).astype(BF)
    puts = []
    for i, (held, out) in enumerate(((hid, hid_hbm), (gg, gg_hbm), (gu, gu_hbm))):
        puts.append(pltpu.make_async_copy(held, out, act_sem.at[i]))
        puts[-1].start()

    def outof(act, held, at):
        return lax.dot_general(act[...], held[at, :], LAST, preferred_element_type=F32)

    count = back_sem.shape[0]
    span = 2 * width // count
    for c in range(count):
        at = slice(c * span, (c + 1) * span)
        if at.start < width:
            part = outof(hid, w_down, at)
        else:
            inner = slice(at.start - width, at.stop - width)
            part = outof(gg, w_gate, inner) + outof(gu, w_up, inner)
        back[:, at] = part.astype(BF)
        puts.append(pltpu.make_async_copy(back.at[:, at], back_hbm.at[:, at], back_sem.at[c]))
        puts[-1].start()
    for put in puts:
        put.wait()


def partial_kernel(parts, base, y_ref, rows_ref, *refs):
    acts, (own_ref, up_ref, dn_ref, up_a, dn_b) = refs[:parts], refs[parts:]
    size = own_ref.shape[0]
    half = size // 2
    y = y_ref[0]
    spots = [(2, 0, up_ref, 0, half), (1, half, up_ref, half, half)]
    spots += [(2, half, dn_ref, 0, half), (3, 0, dn_ref, half, half)]
    spots += [(1, 0, up_a, 0, half), (3, half, dn_b, 0, half), (0, 0, own_ref, 0, size)]
    for j, lead, ref, top, length in spots:
        rows = rows_ref[:, columns(base + lax.rem(y + j, 4) * size + lead, length)]
        at = 0
        for a in acts:
            ref[top : top + length, at : at + a.shape[1]] = lax.dot_general(
                rows, a[...], FIRST, preferred_element_type=F32
            ).astype(BF)
            at += a.shape[1]


def partials(y, rows, base, acts, size):
    wide = sum(a.shape[1] for a in acts)
    full, half = shape_of((size, wide), BF), shape_of((size // 2, wide), BF)
    return whole(
        functools.partial(partial_kernel, len(acts), base),
        [full, full, full, half, half],
        2 + len(acts),
        flops=rows.size * wide,
        nbytes=2 * (rows.size + 4 * size * wide),
        smem=(0,),
        limit=24 * 2**20,
    )(y, rows, *acts)


def sum_kernel(own_ref, up_ref, dn_ref, below_ref, above_ref, *outs):
    half = below_ref.shape[0]
    hidden = outs[0].shape[2]
    for i, out in enumerate(outs):
        at = slice(i * hidden, (i + 1) * hidden)
        out[0, :half] = (
            own_ref[:half, at].astype(F32)
            + below_ref[:, at].astype(F32)
            + dn_ref[half:, at].astype(F32)
        )
        out[0, half:] = (
            own_ref[half:, at].astype(F32)
            + up_ref[half:, at].astype(F32)
            + above_ref[:, at].astype(F32)
        )


def combine_kernel(pieces_ref, pick_ref, rows_ref, out_ref, grad_ref):
    width = out_ref.shape[1]
    rows = rows_ref[:, :width]
    out_ref[...] = added(
        [
            jnp.dot(pieces_ref[i], rows, preferred_element_type=F32)
            for i in range(pieces_ref.shape[0])
        ]
    ).astype(BF)
    grad_ref[...] = jnp.dot(
        pick_ref[...], rows_ref[:, width:], preferred_element_type=F32
    ).astype(BF)


def move_rows(rows, members):
    depth, width = rows.shape
    buffer = rows.reshape(members, depth // members, width)
    moved = lax.all_to_all(buffer, "expert", split_axis=0, concat_axis=0, tiled=True)
    return moved.reshape(depth, width)


def shift(x, by):
    return lax.ppermute(x, "dp", [(i, (i + by) % 4) for i in range(4)])


def ring_gather(weights):
    shard = jnp.concatenate(weights, axis=0)
    half = shard.shape[1] // 2
    below, above = shift(shard, 1), shift(shard, -1)
    far_a = shift(below[:, :half], 1)
    far_b = shift(above[:, half:], -1)
    return below, above, far_a, far_b


def ring_sum(parts, own, up, dn, up_a, dn_b):
    size, wide = own.shape
    half = size // 2
    got_up, got_dn = shift(up, 1), shift(dn, -1)
    up_a = (up_a.astype(F32) + got_up[:half].astype(F32)).astype(BF)
    dn_b = (dn_b.astype(F32) + got_dn[:half].astype(F32)).astype(BF)
    below, above = shift(up_a, 1), shift(dn_b, -1)
    return whole(
        sum_kernel,
        [shape_of((1, size, wide // parts), F32)] * parts,
        5,
        nbytes=12 * size * wide,
        limit=24 * 2**20,
    )(own, got_up, got_dn, below, above)


def shards(
    tokens,
    expert_ids,
    gate_level,
    cost_bucket,
    gate_table,
    gate_weight,
    up_weight,
    down_weight,
    out_grad,
):
    count, width = tokens.shape
    top = expert_ids.shape[1]
    members = lax.axis_size("expert")
    capacity = min(count, 4 * count * top // (3 * members))
    slots = members * capacity
    size, hidden = gate_weight.shape[1:]
    y = lax.axis_index("dp").astype(jnp.int32).reshape(1)

    rows, place, gates = whole(
        functools.partial(send_kernel, members, capacity),
        [
            shape_of((slots, 2 * width), BF),
            shape_of((top, count), jnp.int32),
            shape_of((top, count), F32),
        ],
        6,
        nbytes=6 * 2**20,
        smem=(0, 1),
    )(cost_bucket, gate_table, expert_ids.T, gate_level.T, tokens, out_grad)
    moved = move_rows(rows, members)
    pick, gated = whole(
        pick_kernel,
        [shape_of((count, slots), BF), shape_of((count, slots), F32)],
        2,
        nbytes=2**20,
        limit=16 * 2**20,
    )(place, gates)
    pieces = whole(
        split_kernel, [shape_of((2, count, slots), BF)], 1, nbytes=2**20, limit=16 * 2**20
    )(gated)[0]

    weights = [gate_weight, up_weight, down_weight]
    act = shape_of((slots, hidden), BF)
    any_space = pl.BlockSpec(memory_space=pl.ANY)
    dma = pltpu.SemaphoreType.DMA
    back, hid, grad_gate, grad_up = pl.pallas_call(
        functools.partial(middle_kernel, 256),
        out_shape=[shape_of((slots, 2 * width), BF), act, act, act],
        in_specs=[SMEM] + [any_space] * 8,
        out_specs=[any_space] * 4,
        scratch_shapes=[pltpu.VMEM((slots, 2 * width), BF)]
        + [pltpu.VMEM((width, hidden), BF)] * 3
        + [pltpu.VMEM((slots, 2 * width), BF)]
        + [pltpu.VMEM((slots, hidden), BF)] * 3
        + [dma((2,)), dma((3, 5)), dma((3,)), dma((8,))],
        compiler_params=pltpu.CompilerParams(vmem_limit_bytes=LIMIT),
        cost_estimate=pl.CostEstimate(
            flops=12 * slots * width * hidden, bytes_accessed=20 * 2**20, transcendentals=0
        ),
        name="middle",
    )(y, moved, *weights, *ring_gather(weights))
    returned = move_rows(back, members)

    down_grad = ring_sum(1, *partials(y, moved, width, [hid], size))[0]
    gate_grad, up_grad = ring_sum(2, *partials(y, moved, 0, [grad_gate, grad_up], size))
    output, token_grad = whole(
        combine_kernel, [shape_of((count, width), BF)] * 2, 3, nbytes=6 * 2**20, limit=16 * 2**20
    )(pieces, pick, returned)
    return (output, token_grad, gate_grad, up_grad, down_grad)


def solution(mesh):
    both = ("dp", "expert")
    return jax.shard_map(
        shards,
        mesh=mesh,
        in_specs=(
            P(both, None),
            P(both, None),
            P(both, None),
            P(both),
            P(),
            P("expert", "dp", None),
            P("expert", "dp", None),
            P("expert", "dp", None),
            P(both, None),
        ),
        out_specs=(
            P(both, None),
            P(both, None),
            P("expert", "dp", None),
            P("expert", "dp", None),
            P("expert", "dp", None),
        ),
        check_vma=False,
    )
```

time: 347 us -> 238 us (0.69)
  waiting for transfers between devices: 211 us -> 157 us
  Pallas kernels: 62.9 us -> 38.9 us
  starting transfers between devices: 55.2 us -> 37.5 us
  local copies, waits for them, and re-layouts: 8.95 us -> 2.68 us
  other arithmetic: 6.42 us -> 0.56 us
    all_to_all x4 -> x2, waiting for transfers between devices: 82.8 us -> 17.6 us  [move_rows(): lax.all_to_all(buffer, 'expert', split_axis=0, concat_axis=0, tiled=True)]
    pallas_call x10 -> x5, Pallas kernels: 51 us -> 30.6 us  [the longest x1 16.7 us: shards(): pl.pallas_call(functools.partial(middle_kernel, 256), out_shape=[shape_of...]
    all_to_all x4 -> x2, starting transfers between devices: 38.1 us -> 19.4 us  [move_rows(): lax.all_to_all(buffer, 'expert', split_axis=0, concat_axis=0, tiled=True)]
    ppermute x12, waiting for transfers between devices: 128 us -> 139 us  [shift(): return lax.ppermute(x, 'dp', [(i, (i + by) % 4) for i in range(4)])]
    unnamed x32 -> x24, local copies, waits for them, and re-layouts: 8.74 us -> 2.47 us
    pallas_call x2, Pallas kernels: 6.91 us -> 3.32 us  [ring_sum(): whole(sum_kernel, [shape_of((1, size, wide // parts), F32)] * parts, 5, n...]
  transfers between devices with their start and end apart: 16 -> 14, of which waited for: 8 -> 8; matrix products, arithmetic and copies ran while one was open for 2% -> 0% of each run, Pallas kernels for 16% -> 6%
where the time goes in v2:
time: 238 us; the launch traced here: 237 us
  waiting for transfers between devices  157 us (66%)
  Pallas kernels  38.9 us (16%)
  starting transfers between devices  37.5 us (16%)
  local copies, waits for them, and re-layouts  2.68 us (1%)
    ppermute x12, waiting for transfers between devices, shift(): return lax.ppermute(x, 'dp', [(i, (i + by) % 4) for i in range(4)])  139 us
    all_to_all x2, starting transfers between devices, move_rows(): lax.all_to_all(buffer, 'expert', split_axis=0, concat_axis=0, tiled=True)  19.4 us
    ppermute x12, starting transfers between devices, shift(): return lax.ppermute(x, 'dp', [(i, (i + by) % 4) for i in range(4)])  18.2 us
    all_to_all x2, waiting for transfers between devices, move_rows(): lax.all_to_all(buffer, 'expert', split_axis=0, concat_axis=0, tiled=True)  17.6 us
    pallas_call x1, Pallas kernels, shards(): pl.pallas_call(functools.partial(middle_kernel, 256), out_shape=[shape_of...  16.7 us
    pallas_call x2, Pallas kernels, partials(): whole(functools.partial(partial_kernel, len(acts), base), [full, full, fu...  9.77 us
  transfers between devices with their start and end apart: 14, of which 8 were waited for; matrix products, arithmetic and copies ran while one was open for 0% of the time, Pallas kernels for 6%

profile of v2, /device:TPU:1, one launch (start us, length us, event | category | flops | bytes accessed | tf_op | source)
XLA Modules:
  0.0 237.3 jit_solution(3502916800895518919)
XLA Ops:
  0.6 4.7 %shard_map.128 = (bf16[512,4096]{1,0:T(8,128)(2,1)}, s32[3,128]{1,0:T(4,128)}, f32[3,128]{1,0:T(4,128)}) custom-call(s32[2]{0:T(128)} %bucket_ref.1, f32[8,16]{1,0:T(8,128)} %table_ref.1, s32[3,128]{1,0:T(4,128)} %bitcast.9, s32[3,128]{1,0:T(4,128)} %bitcast.10, bf16[128,2048]{1,0:T(8,128)(2,1)} %tokens_ref.1, bf16[128,2048]{1,0:T(8,128)(2,1)} %grad_ref.1), custom_call_target="tpu_custom_call" | custom-call | bytes 6291456 | tf_op jit(solution)/shard_map/pallas_call | solution.py:339
  5.4 0.0 copy-start.5
  5.4 13.3 %all-to-all-start = ((bf16[64,8,4096]{2,1,0:T(8,128)(2,1)}), bf16[64,8,4096]{2,1,0:T(8,128)(2,1)}, u32[]{:S(2)}, u32[]{:S(2)}) async-start(bf16[64,8,4096]{2,1,0:T(8,128)(2,1)} %bitcast.8), calls=%async_computation | async-start | bytes 8388608 | tf_op jit(solution)/shard_map/all_to_all | solution.py:287
  18.7 0.0 copy-done.5
  18.7 0.0 copy-start.6
  18.7 0.0 copy-start.7
  18.7 0.1 constant_dynamic-update-slice_fusion.2
  18.8 1.1 copy-done.6
  19.8 0.1 constant_dynamic-update-slice_fusion.1
  19.9 0.2 copy-done.7
  20.1 0.1 constant_dynamic-update-slice_fusion
  20.1 2.8 %collective-permute-start.1 = (bf16[3,512,768]{2,1,0:T(8,128)(2,1)S(1)}, bf16[3,512,768]{2,1,0:T(8,128)(2,1)S(1)}, u32[]{:S(2)}, u32[]{:S(2)}) collective-permute-start(bf16[3,512,768]{2,1,0:T(8,128)(2,1)S(1)} %constant_dynamic-update-slice_fusion), channel_id=1, source_target_pairs={{0,192},{64,0},{128,64},{192,128},{1,193},{65,1},{129,65},{193,129... | collective-permute-start | bytes 7077896 | tf_op jit(solution)/shard_map/ppermute | solution.py:292
  22.9 0.0 collective-permute-start
  22.9 50.1 %collective-permute-done.1.above = bf16[3,512,768]{2,1,0:T(8,128)(2,1)S(1)} collective-permute-done((bf16[3,512,768]{2,1,0:T(8,128)(2,1)S(1)}, bf16[3,512,768]{2,1,0:T(8,128)(2,1)S(1)}, u32[]{:S(2)}, u32[]{:S(2)}) %collective-permute-start.1) | collective-permute-done | bytes 2359328 | tf_op jit(solution)/shard_map/ppermute | solution.py:292
  73.0 0.1 slice.25
  73.1 3.6 %collective-permute-start.3 = (bf16[3,256,768]{2,1,0:T(8,128)(2,1)S(1)}, bf16[3,256,768]{2,1,0:T(8,128)(2,1)S(1)}, u32[]{:S(2)}, u32[]{:S(2)}) collective-permute-start(bf16[3,256,768]{2,1,0:T(8,128)(2,1)S(1)} %slice.25), channel_id=1, source_target_pairs={{0,192},{64,0},{128,64},{192,128},{1,193},{65,1},{129,65},{193,129... | collective-permute-start | bytes 3538952 | tf_op jit(solution)/shard_map/ppermute | solution.py:292
  76.7 0.0 collective-permute-done.below
  76.7 0.1 slice.24
  76.8 0.0 copy-done.8
  76.8 0.3 collective-permute-start.2
  77.0 1.1 copy-done.9
  78.1 22.6 %collective-permute-done.3.far_b = bf16[3,256,768]{2,1,0:T(8,128)(2,1)S(1)} collective-permute-done((bf16[3,256,768]{2,1,0:T(8,128)(2,1)S(1)}, bf16[3,256,768]{2,1,0:T(8,128)(2,1)S(1)}, u32[]{:S(2)}, u32[]{:S(2)}) %collective-permute-start.3) | collective-permute-done | bytes 1179680 | tf_op jit(solution)/shard_map/ppermute | solution.py:292
  100.7 3.6 %collective-permute-done.2.far_a = bf16[3,256,768]{2,1,0:T(8,128)(2,1)} collective-permute-done((bf16[3,256,768]{2,1,0:T(8,128)(2,1)S(1)}, bf16[3,256,768]{2,1,0:T(8,128)(2,1)}, u32[]{:S(2)}, u32[]{:S(2)}) %collective-permute-start.2) | collective-permute-done | bytes 1179680 | tf_op jit(solution)/shard_map/ppermute | solution.py:292
  104.3 0.0 copy-done.10
  104.3 10.2 %all-to-all-done = bf16[64,8,4096]{2,1,0:T(8,128)(2,1)} async-done(((bf16[64,8,4096]{2,1,0:T(8,128)(2,1)}), bf16[64,8,4096]{2,1,0:T(8,128)(2,1)}, u32[]{:S(2)}, u32[]{:S(2)}) %all-to-all-start) | async-done | bytes 4194336 | tf_op jit(solution)/shard_map/all_to_all | solution.py:287
  114.5 16.7 %middle.1 = (bf16[512,4096]{1,0:T(8,128)(2,1)}, bf16[512,768]{1,0:T(8,128)(2,1)}, bf16[512,768]{1,0:T(8,128)(2,1)}, bf16[512,768]{1,0:T(8,128)(2,1)}) custom-call(s32[1]{0:T(128)} %bitcast.2.y_ref, bf16[512,4096]{1,0:T(8,128)(2,1)} %bitcast.4.rows_hbm.rows_ref, bf16[1,512,768]{2,1,0:T(8,128)(2,1)} %gate_w.1, bf16[1,512,768]{2,1,0:T(8,128)(2,1)} %up_w.1, ...), custom_call_target="tpu_custom_call" | custom-call | flops 9663676416 | bytes 20971520 | tf_op jit(solution)/shard_map/middle/pallas_call | solution.py:366
  131.3 0.0 copy-start.3
  131.3 0.0 copy-start.4
  131.3 6.1 %all-to-all-start.1 = ((bf16[64,8,4096]{2,1,0:T(8,128)(2,1)}), bf16[64,8,4096]{2,1,0:T(8,128)(2,1)}, u32[]{:S(2)}, u32[]{:S(2)}) async-start(bf16[64,8,4096]{2,1,0:T(8,128)(2,1)} %bitcast.7), calls=%async_computation.1 | async-start | bytes 8388608 | tf_op jit(solution)/shard_map/all_to_all | solution.py:287
  137.4 0.0 copy-done.3
  137.4 0.0 copy-done.4
  137.4 0.0 copy-start.2
  137.4 5.7 %shard_map.132 = (bf16[512,1536]{1,0:T(8,128)(2,1)S(1)}, bf16[512,1536]{1,0:T(8,128)(2,1)S(1)}, bf16[512,1536]{1,0:T(8,128)(2,1)S(1)}, bf16[256,1536]{1,0:T(8,128)(2,1)S(1)}, bf16[256,1536]{1,0:T(8,128)(2,1)S(1)}) custom-call(s32[1]{0:T(128)} %bitcast.2.y_ref, bf16[512,4096]{1,0:T(8,128)(2,1)} %bitcast.4.rows_hbm.rows_ref, bf16[512,768]{1,0:T(8,128)(2,1)S(1)} %copy-done.3, ...), custom_call_target="tpu_custom_call" | custom-call | flops 3221225472 | bytes 10485760 | tf_op jit(solution)/shard_map/pallas_call | solution.py:242
  143.2 1.6 collective-permute-start.4
  144.8 1.5 collective-permute-start.5
  146.3 0.0 copy-done.2
  146.3 4.0 %shard_map.134 = (bf16[512,768]{1,0:T(8,128)(2,1)S(1)}, bf16[512,768]{1,0:T(8,128)(2,1)S(1)}, bf16[512,768]{1,0:T(8,128)(2,1)S(1)}, bf16[256,768]{1,0:T(8,128)(2,1)S(1)}, bf16[256,768]{1,0:T(8,128)(2,1)S(1)}) custom-call(s32[1]{0:T(128)} %bitcast.2.y_ref, bf16[512,4096]{1,0:T(8,128)(2,1)} %bitcast.4.rows_hbm.rows_ref, bf16[512,768]{1,0:T(8,128)(2,1)S(1)} %copy-done.2), custom_call_target="tpu_custom_call" | custom-call | flops 1610612736 | bytes 7340032 | tf_op jit(solution)/shard_map/pallas_call | solution.py:242
  150.3 0.1 collective-permute-start.8
  150.4 2.7 %collective-permute-start.9 = (bf16[512,768]{1,0:T(8,128)(2,1)S(1)}, bf16[512,768]{1,0:T(8,128)(2,1)S(1)}, u32[]{:S(2)}, u32[]{:S(2)}) collective-permute-start(bf16[512,768]{1,0:T(8,128)(2,1)S(1)} %get-tuple-element.48), channel_id=1, source_target_pairs={{0,192},{64,0},{128,64},{192,128},{1,193},{65,1},{129,65},{193,129... | collective-permute-start | bytes 2359304 | tf_op jit(solution)/shard_map/ppermute | solution.py:292
  153.1 27.1 %collective-permute-done.4.up_ref = bf16[512,1536]{1,0:T(8,128)(2,1)S(1)} collective-permute-done((bf16[512,1536]{1,0:T(8,128)(2,1)S(1)}, bf16[512,1536]{1,0:T(8,128)(2,1)S(1)}, u32[]{:S(2)}, u32[]{:S(2)}) %collective-permute-start.4) | collective-permute-done | bytes 1572896 | tf_op jit(solution)/shard_map/ppermute | solution.py:292
  180.2 0.2 add_convert_fusion.1
  180.4 0.1 collective-permute-start.6
  180.5 0.0 collective-permute-done.5.dn_ref
  180.5 0.2 add_convert_fusion
  180.7 0.0 copy-start
  180.7 0.0 copy-start.1
  180.8 2.7 %collective-permute-start.7 = (bf16[256,1536]{1,0:T(8,128)(2,1)S(1)}, bf16[256,1536]{1,0:T(8,128)(2,1)S(1)}, u32[]{:S(2)}, u32[]{:S(2)}) collective-permute-start(bf16[256,1536]{1,0:T(8,128)(2,1)S(1)} %add_convert_fusion), channel_id=1, source_target_pairs={{0,192},{64,0},{128,64},{192,128},{1,193},{65,1},{129,65},{193,129... | collective-permute-start | bytes 2359304 | tf_op jit(solution)/shard_map/ppermute | solution.py:292
  183.5 13.7 %collective-permute-done.8.up_ref = bf16[512,768]{1,0:T(8,128)(2,1)S(1)} collective-permute-done((bf16[512,768]{1,0:T(8,128)(2,1)S(1)}, bf16[512,768]{1,0:T(8,128)(2,1)S(1)}, u32[]{:S(2)}, u32[]{:S(2)}) %collective-permute-start.8) | collective-permute-done | bytes 786464 | tf_op jit(solution)/shard_map/ppermute | solution.py:292
  197.2 0.1 add_convert_fusion.3
  197.3 0.1 collective-permute-start.10
  197.4 0.0 collective-permute-done.9.dn_ref
  197.4 0.1 add_convert_fusion.2
  197.5 2.7 %collective-permute-start.11 = (bf16[256,768]{1,0:T(8,128)(2,1)S(1)}, bf16[256,768]{1,0:T(8,128)(2,1)S(1)}, u32[]{:S(2)}, u32[]{:S(2)}) collective-permute-start(bf16[256,768]{1,0:T(8,128)(2,1)S(1)} %add_convert_fusion.2), channel_id=1, source_target_pairs={{0,192},{64,0},{128,64},{192,128},{1,193},{65,1},{129,65},{193,129... | collective-permute-start | bytes 1179656 | tf_op jit(solution)/shard_map/ppermute | solution.py:292
  200.2 0.0 copy-done
  200.2 0.0 copy-done.1
  200.2 0.3 shard_map.129
  200.6 21.9 %collective-permute-done.10.below_ref = bf16[256,768]{1,0:T(8,128)(2,1)S(1)} collective-permute-done((bf16[256,768]{1,0:T(8,128)(2,1)S(1)}, bf16[256,768]{1,0:T(8,128)(2,1)S(1)}, u32[]{:S(2)}, u32[]{:S(2)}) %collective-permute-start.10) | collective-permute-done | bytes 393248 | tf_op jit(solution)/shard_map/ppermute | solution.py:292
  222.5 0.0 collective-permute-done.11.above_ref
  222.5 1.4 shard_map.135
  223.9 0.0 collective-permute-done.6.below_ref
  223.9 0.0 collective-permute-done.7.above_ref
  223.9 1.9 shard_map.133
  225.8 7.4 %all-to-all-done.1 = bf16[64,8,4096]{2,1,0:T(8,128)(2,1)} async-done(((bf16[64,8,4096]{2,1,0:T(8,128)(2,1)}), bf16[64,8,4096]{2,1,0:T(8,128)(2,1)}, u32[]{:S(2)}, u32[]{:S(2)}) %all-to-all-start.1) | async-done | bytes 4194336 | tf_op jit(solution)/shard_map/all_to_all | solution.py:287
  233.2 4.0 %shard_map.131 = (bf16[128,2048]{1,0:T(8,128)(2,1)}, bf16[128,2048]{1,0:T(8,128)(2,1)}) custom-call(bf16[2,128,512]{2,1,0:T(8,128)(2,1)S(1)} %shard_map.130.pieces_ref, bf16[128,512]{1,0:T(8,128)(2,1)S(1)} %get-tuple-element.31.pick_ref, bf16[512,4096]{1,0:T(8,128)(2,1)} %bitcast.6.rows_ref), custom_call_target="tpu_custom_call" | custom-call | bytes 6291456 | tf_op jit(solution)/shard_map/pallas_call | solution.py:386
  (4 shorter events, 0.0 us)
Async XLA Ops:
  5.4 13.3 %copy-start.5 = (bf16[1,512,768]{2,1,0:T(8,128)(2,1)S(1)}, bf16[1,512,768]{2,1,0:T(8,128)(2,1)}, u32[]{:S(2)}) copy-start(bf16[1,512,768]{2,1,0:T(8,128)(2,1)} %gate_w.1) | copy-start | bytes 2359300
  5.4 109.2 %all-to-all-start = ((bf16[64,8,4096]{2,1,0:T(8,128)(2,1)}), bf16[64,8,4096]{2,1,0:T(8,128)(2,1)}, u32[]{:S(2)}, u32[]{:S(2)}) async-start(bf16[64,8,4096]{2,1,0:T(8,128)(2,1)} %bitcast.8), calls=%async_computation | async-start | bytes 8388608 | tf_op jit(solution)/shard_map/all_to_all | solution.py:287
  18.7 1.1 copy-start.6
  18.7 1.4 copy-start.7
  20.1 52.9 %collective-permute-start.1 = (bf16[3,512,768]{2,1,0:T(8,128)(2,1)S(1)}, bf16[3,512,768]{2,1,0:T(8,128)(2,1)S(1)}, u32[]{:S(2)}, u32[]{:S(2)}) collective-permute-start(bf16[3,512,768]{2,1,0:T(8,128)(2,1)S(1)} %constant_dynamic-update-slice_fusion), channel_id=1, source_target_pairs={{0,192},{64,0},{128,64},{192,128},{1,193},{65,1},{129,65},{193,129... | collective-permute-start | bytes 7077896 | tf_op jit(solution)/shard_map/ppermute | solution.py:292
  22.9 53.8 %collective-permute-start = (bf16[3,512,768]{2,1,0:T(8,128)(2,1)S(1)}, bf16[3,512,768]{2,1,0:T(8,128)(2,1)S(1)}, u32[]{:S(2)}, u32[]{:S(2)}) collective-permute-start(bf16[3,512,768]{2,1,0:T(8,128)(2,1)S(1)} %constant_dynamic-update-slice_fusion), channel_id=1, source_target_pairs={{0,64},{64,128},{128,192},{192,0},{1,65},{65,129},{129,193},{193,1... | collective-permute-start | bytes 7077896 | tf_op jit(solution)/shard_map/ppermute | solution.py:292
  73.0 3.8 %copy-start.8 = (bf16[3,512,768]{2,1,0:T(8,128)(2,1)}, bf16[3,512,768]{2,1,0:T(8,128)(2,1)S(1)}, u32[]{:S(2)}) copy-start(bf16[3,512,768]{2,1,0:T(8,128)(2,1)S(1)} %collective-permute-done.1.above) | copy-start | bytes 7077892
  73.1 27.6 %collective-permute-start.3 = (bf16[3,256,768]{2,1,0:T(8,128)(2,1)S(1)}, bf16[3,256,768]{2,1,0:T(8,128)(2,1)S(1)}, u32[]{:S(2)}, u32[]{:S(2)}) collective-permute-start(bf16[3,256,768]{2,1,0:T(8,128)(2,1)S(1)} %slice.25), channel_id=1, source_target_pairs={{0,192},{64,0},{128,64},{192,128},{1,193},{65,1},{129,65},{193,129... | collective-permute-start | bytes 3538952 | tf_op jit(solution)/shard_map/ppermute | solution.py:292
  76.7 1.4 copy-start.9
  76.8 27.5 %collective-permute-start.2 = (bf16[3,256,768]{2,1,0:T(8,128)(2,1)S(1)}, bf16[3,256,768]{2,1,0:T(8,128)(2,1)}, u32[]{:S(2)}, u32[]{:S(2)}) collective-permute-start(bf16[3,256,768]{2,1,0:T(8,128)(2,1)S(1)} %slice.24), channel_id=1, source_target_pairs={{0,64},{64,128},{128,192},{192,0},{1,65},{65,129},{129,193},{193,1... | collective-permute-start | bytes 3538952 | tf_op jit(solution)/shard_map/ppermute | solution.py:292
  100.7 3.6 %copy-start.10 = (bf16[3,256,768]{2,1,0:T(8,128)(2,1)}, bf16[3,256,768]{2,1,0:T(8,128)(2,1)S(1)}, u32[]{:S(2)}) copy-start(bf16[3,256,768]{2,1,0:T(8,128)(2,1)S(1)} %collective-permute-done.3.far_b) | copy-start | bytes 3538948
  131.3 6.1 %copy-start.3 = (bf16[512,768]{1,0:T(8,128)(2,1)S(1)}, bf16[512,768]{1,0:T(8,128)(2,1)}, u32[]{:S(2)}) copy-start(bf16[512,768]{1,0:T(8,128)(2,1)} %get-tuple-element.36.refs_0_) | copy-start | bytes 2359300
  131.3 6.1 %copy-start.4 = (bf16[512,768]{1,0:T(8,128)(2,1)S(1)}, bf16[512,768]{1,0:T(8,128)(2,1)}, u32[]{:S(2)}) copy-start(bf16[512,768]{1,0:T(8,128)(2,1)} %get-tuple-element.37.refs_1_) | copy-start | bytes 2359300
  131.3 101.9 %all-to-all-start.1 = ((bf16[64,8,4096]{2,1,0:T(8,128)(2,1)}), bf16[64,8,4096]{2,1,0:T(8,128)(2,1)}, u32[]{:S(2)}, u32[]{:S(2)}) async-start(bf16[64,8,4096]{2,1,0:T(8,128)(2,1)} %bitcast.7), calls=%async_computation.1 | async-start | bytes 8388608 | tf_op jit(solution)/shard_map/all_to_all | solution.py:287
  137.4 8.9 %copy-start.2 = (bf16[512,768]{1,0:T(8,128)(2,1)S(1)}, bf16[512,768]{1,0:T(8,128)(2,1)}, u32[]{:S(2)}) copy-start(bf16[512,768]{1,0:T(8,128)(2,1)} %get-tuple-element.45.refs_0_) | copy-start | bytes 2359300
  143.2 37.1 %collective-permute-start.4 = (bf16[512,1536]{1,0:T(8,128)(2,1)S(1)}, bf16[512,1536]{1,0:T(8,128)(2,1)S(1)}, u32[]{:S(2)}, u32[]{:S(2)}) collective-permute-start(bf16[512,1536]{1,0:T(8,128)(2,1)S(1)} %get-tuple-element.39), channel_id=1, source_target_pairs={{0,64},{64,128},{128,192},{192,0},{1,65},{65,129},{129,193},{193,1... | collective-permute-start | bytes 4718600 | tf_op jit(solution)/shard_map/ppermute | solution.py:292
  144.8 35.8 %collective-permute-start.5 = (bf16[512,1536]{1,0:T(8,128)(2,1)S(1)}, bf16[512,1536]{1,0:T(8,128)(2,1)S(1)}, u32[]{:S(2)}, u32[]{:S(2)}) collective-permute-start(bf16[512,1536]{1,0:T(8,128)(2,1)S(1)} %get-tuple-element.40), channel_id=1, source_target_pairs={{0,192},{64,0},{128,64},{192,128},{1,193},{65,1},{129,65},{193,129... | collective-permute-start | bytes 4718600 | tf_op jit(solution)/shard_map/ppermute | solution.py:292
  150.3 46.9 %collective-permute-start.8 = (bf16[512,768]{1,0:T(8,128)(2,1)S(1)}, bf16[512,768]{1,0:T(8,128)(2,1)S(1)}, u32[]{:S(2)}, u32[]{:S(2)}) collective-permute-start(bf16[512,768]{1,0:T(8,128)(2,1)S(1)} %get-tuple-element.47), channel_id=1, source_target_pairs={{0,64},{64,128},{128,192},{192,0},{1,65},{65,129},{129,193},{193,1... | collective-permute-start | bytes 2359304 | tf_op jit(solution)/shard_map/ppermute | solution.py:292
  150.4 47.0 %collective-permute-start.9 = (bf16[512,768]{1,0:T(8,128)(2,1)S(1)}, bf16[512,768]{1,0:T(8,128)(2,1)S(1)}, u32[]{:S(2)}, u32[]{:S(2)}) collective-permute-start(bf16[512,768]{1,0:T(8,128)(2,1)S(1)} %get-tuple-element.48), channel_id=1, source_target_pairs={{0,192},{64,0},{128,64},{192,128},{1,193},{65,1},{129,65},{193,129... | collective-permute-start | bytes 2359304 | tf_op jit(solution)/shard_map/ppermute | solution.py:292
  180.4 43.5 %collective-permute-start.6 = (bf16[256,1536]{1,0:T(8,128)(2,1)S(1)}, bf16[256,1536]{1,0:T(8,128)(2,1)S(1)}, u32[]{:S(2)}, u32[]{:S(2)}) collective-permute-start(bf16[256,1536]{1,0:T(8,128)(2,1)S(1)} %add_convert_fusion.1), channel_id=1, source_target_pairs={{0,64},{64,128},{128,192},{192,0},{1,65},{65,129},{129,193},{193,1... | collective-permute-start | bytes 2359304 | tf_op jit(solution)/shard_map/ppermute | solution.py:292
  180.7 19.5 %copy-start = (s32[3,128]{1,0:T(4,128)S(1)}, s32[3,128]{1,0:T(4,128)}, u32[]{:S(2)}) copy-start(s32[3,128]{1,0:T(4,128)} %get-tuple-element.28.place_ref) | copy-start | bytes 4612
  180.7 19.5 %copy-start.1 = (f32[3,128]{1,0:T(4,128)S(1)}, f32[3,128]{1,0:T(4,128)}, u32[]{:S(2)}) copy-start(f32[3,128]{1,0:T(4,128)} %get-tuple-element.29.gate_ref) | copy-start | bytes 4612
  180.8 43.1 %collective-permute-start.7 = (bf16[256,1536]{1,0:T(8,128)(2,1)S(1)}, bf16[256,1536]{1,0:T(8,128)(2,1)S(1)}, u32[]{:S(2)}, u32[]{:S(2)}) collective-permute-start(bf16[256,1536]{1,0:T(8,128)(2,1)S(1)} %add_convert_fusion), channel_id=1, source_target_pairs={{0,192},{64,0},{128,64},{192,128},{1,193},{65,1},{129,65},{193,129... | collective-permute-start | bytes 2359304 | tf_op jit(solution)/shard_map/ppermute | solution.py:292
  197.3 25.2 %collective-permute-start.10 = (bf16[256,768]{1,0:T(8,128)(2,1)S(1)}, bf16[256,768]{1,0:T(8,128)(2,1)S(1)}, u32[]{:S(2)}, u32[]{:S(2)}) collective-permute-start(bf16[256,768]{1,0:T(8,128)(2,1)S(1)} %add_convert_fusion.3), channel_id=1, source_target_pairs={{0,64},{64,128},{128,192},{192,0},{1,65},{65,129},{129,193},{193,1... | collective-permute-start | bytes 1179656 | tf_op jit(solution)/shard_map/ppermute | solution.py:292
  197.5 25.0 %collective-permute-start.11 = (bf16[256,768]{1,0:T(8,128)(2,1)S(1)}, bf16[256,768]{1,0:T(8,128)(2,1)S(1)}, u32[]{:S(2)}, u32[]{:S(2)}) collective-permute-start(bf16[256,768]{1,0:T(8,128)(2,1)S(1)} %add_convert_fusion.2), channel_id=1, source_target_pairs={{0,192},{64,0},{128,64},{192,128},{1,193},{65,1},{129,65},{193,129... | collective-permute-start | bytes 1179656 | tf_op jit(solution)/shard_map/ppermute | solution.py:292

commit v3 on v2

--- a/solution.py
+++ b/solution.py
@@ -106,9 +106,10 @@
 
 def split_kernel(gated_ref, pieces_ref):
     rest = gated_ref[...]
-    for i in range(pieces_ref.shape[0]):
+    count = rest.shape[0]
+    for at in range(0, pieces_ref.shape[0], count):
         piece = rest.astype(BF)
-        pieces_ref[i] = piece
+        pieces_ref[at : at + count] = piece
         rest = rest - piece.astype(F32)
 
 
@@ -145,6 +146,8 @@
     hid,
     gg,
     gu,
+    gate_out,
+    up_out,
     row_sem,
     weight_sem,
     act_sem,
@@ -152,43 +155,57 @@
 ):
     hidden = hid.shape[1]
     width = rows.shape[1] // 2
-    spots = offsets(y_ref[0], 4, width // 4)
-
-    def fetch_rows(part):
-        at = slice(part * width, (part + 1) * width)
-        copy = pltpu.make_async_copy(rows_hbm.at[:, at], rows.at[:, at], row_sem.at[part])
+    quarter = width // 4
+    spots = offsets(y_ref[0], 4, quarter)
+    tiles = [slice(at, at + tile) for at in range(0, hidden, tile)]
+
+    def begin(source, held, sem):
+        copy = pltpu.make_async_copy(source, held, sem)
         copy.start()
-        return [copy]
-
-    def fetch_weight(i, shard, held):
+        return copy
+
+    def fetch_weight(i, shard, held, chosen_pieces):
         sources = [shard.at[0]] + [ref.at[i] for ref in (below, above, far_a, far_b)]
-        copies = [
-            pltpu.make_async_copy(
-                source, held.at[pl.ds(pl.multiple_of(off, 256), size), :], weight_sem.at[i, j]
+        return [
+            begin(
+                sources[j],
+                held.at[pl.ds(pl.multiple_of(spots[j][0], 256), spots[j][1]), :],
+                weight_sem.at[i, j],
             )
-            for j, (source, (off, size)) in enumerate(zip(sources, spots))
+            for j in chosen_pieces
         ]
-        for copy in copies:
-            copy.start()
-        return copies
-
-    waits = [
-        fetch_rows(0) + fetch_weight(0, gate_w, w_gate),
-        fetch_weight(1, up_w, w_up),
-        fetch_rows(1) + fetch_weight(2, down_w, w_down),
-    ]
-    tiles = [slice(at, at + tile) for at in range(0, hidden, tile)]
-
-    def into(i, base, held, at):
-        if at.start == 0:
-            for copy in waits[i]:
-                copy.wait()
-        return jnp.dot(rows[:, base : base + width], held[:, at], preferred_element_type=F32)
-
+
+    chunks = [(0,), (1,), (2,), (3, 4)]
+    arrivals = []
+    for c, chunk in enumerate(chunks):
+        at = columns(spots[chunk[0]][0], quarter)
+        arrivals.append(
+            [begin(rows_hbm.at[:, at], rows.at[:, at], row_sem.at[c])]
+            + fetch_weight(0, gate_w, w_gate, chunk)
+            + fetch_weight(1, up_w, w_up, chunk)
+        )
+    late = [
+        begin(rows_hbm.at[:, width:], rows.at[:, width:], row_sem.at[len(chunks)])
+    ] + fetch_weight(2, down_w, w_down, range(5))
+
+    for c, chunk in enumerate(chunks):
+        for copy in arrivals[c]:
+            copy.wait()
+        off = spots[chunk[0]][0]
+        some = rows[:, columns(off, quarter)]
+        for held, out in ((w_gate, gate_out), (w_up, up_out)):
+            for at in tiles:
+                part = jnp.dot(
+                    some,
+                    held[pl.ds(pl.multiple_of(off, 512), quarter), at],
+                    preferred_element_type=F32,
+                )
+                out[:, at] = part if c == 0 else out[:, at] + part
+    for copy in late:
+        copy.wait()
     for at in tiles:
-        gate_act = into(0, 0, w_gate, at)
-        up_act = into(1, 0, w_up, at)
-        grad = into(2, width, w_down, at)
+        grad = jnp.dot(rows[:, width:], w_down[:, at], preferred_element_type=F32)
+        gate_act, up_act = gate_out[:, at], up_out[:, at]
         s = jax.nn.sigmoid(gate_act)
         swish = gate_act * s
         hid[:, at] = (swish * up_act).astype(BF)
@@ -268,13 +285,10 @@
 
 
 def combine_kernel(pieces_ref, pick_ref, rows_ref, out_ref, grad_ref):
-    width = out_ref.shape[1]
-    rows = rows_ref[:, :width]
+    count, width = out_ref.shape
+    parts = jnp.dot(pieces_ref[...], rows_ref[:, :width], preferred_element_type=F32)
     out_ref[...] = added(
-        [
-            jnp.dot(pieces_ref[i], rows, preferred_element_type=F32)
-            for i in range(pieces_ref.shape[0])
-        ]
+        [parts[at : at + count] for at in range(0, parts.shape[0], count)]
     ).astype(BF)
     grad_ref[...] = jnp.dot(
         pick_ref[...], rows_ref[:, width:], preferred_element_type=F32
@@ -356,7 +370,11 @@
         limit=16 * 2**20,
     )(place, gates)
     pieces = whole(
-        split_kernel, [shape_of((2, count, slots), BF)], 1, nbytes=2**20, limit=16 * 2**20
+        split_kernel,
+        [shape_of((2 * count, slots), BF)],
+        1,
+        nbytes=2**20,
+        limit=16 * 2**20,
     )(gated)[0]
 
     weights = [gate_weight, up_weight, down_weight]
@@ -372,7 +390,8 @@
         + [pltpu.VMEM((width, hidden), BF)] * 3
         + [pltpu.VMEM((slots, 2 * width), BF)]
         + [pltpu.VMEM((slots, hidden), BF)] * 3
-        + [dma((2,)), dma((3, 5)), dma((3,)), dma((8,))],
+        + [pltpu.VMEM((slots, hidden), F32)] * 2
+        + [dma((5,)), dma((3, 5)), dma((3,)), dma((16,))],
         compiler_params=pltpu.CompilerParams(vmem_limit_bytes=LIMIT),
         cost_estimate=pl.CostEstimate(
             flops=12 * slots * width * hidden, bytes_accessed=20 * 2**20, transcendentals=0
@@ -384,7 +403,11 @@
     down_grad = ring_sum(1, *partials(y, moved, width, [hid], size))[0]
     gate_grad, up_grad = ring_sum(2, *partials(y, moved, 0, [grad_gate, grad_up], size))
     output, token_grad = whole(
-        combine_kernel, [shape_of((count, width), BF)] * 2, 3, nbytes=6 * 2**20, limit=16 * 2**20
+        combine_kernel,
+        [shape_of((count, width), BF)] * 2,
+        3,
+        nbytes=6 * 2**20,
+        limit=16 * 2**20,
     )(pieces, pick, returned)
     return (output, token_grad, gate_grad, up_grad, down_grad)
 

time: 238 us -> 236 us (level)
  no operation moved by 1% of the time
where the time goes in v3:
time: 236 us; the launch traced here: 235 us
  waiting for transfers between devices  157 us (67%)
  starting transfers between devices  37.4 us (16%)
  Pallas kernels  37.1 us (16%)
  local copies, waits for them, and re-layouts  2.68 us (1%)
    ppermute x12, waiting for transfers between devices, shift(): return lax.ppermute(x, 'dp', [(i, (i + by) % 4) for i in range(4)])  139 us
    all_to_all x2, starting transfers between devices, move_rows(): lax.all_to_all(buffer, 'expert', split_axis=0, concat_axis=0, tiled=True)  19.4 us
    all_to_all x2, waiting for transfers between devices, move_rows(): lax.all_to_all(buffer, 'expert', split_axis=0, concat_axis=0, tiled=True)  18 us
    ppermute x12, starting transfers between devices, shift(): return lax.ppermute(x, 'dp', [(i, (i + by) % 4) for i in range(4)])  18 us
    pallas_call x1, Pallas kernels, shards(): pl.pallas_call(functools.partial(middle_kernel, 256), out_shape=[shape_of...  15 us
    pallas_call x2, Pallas kernels, partials(): whole(functools.partial(partial_kernel, len(acts), base), [full, full, fu...  9.77 us
    pallas_call x1, Pallas kernels, shards(): whole(functools.partial(send_kernel, members, capacity), [shape_of((slots...  4.73 us
  transfers between devices with their start and end apart: 14, of which 8 were waited for; matrix products, arithmetic and copies ran while one was open for 0% of the time, Pallas kernels for 6%

profile of v3, /device:TPU:1, one launch (start us, length us, event | category | flops | bytes accessed | tf_op | source)
XLA Modules:
  0.0 235.4 jit_solution(3979493398355322711)
XLA Ops:
  0.6 4.7 %shard_map.128 = (bf16[512,4096]{1,0:T(8,128)(2,1)}, s32[3,128]{1,0:T(4,128)}, f32[3,128]{1,0:T(4,128)}) custom-call(s32[2]{0:T(128)} %bucket_ref.1, f32[8,16]{1,0:T(8,128)} %table_ref.1, s32[3,128]{1,0:T(4,128)} %bitcast.9, s32[3,128]{1,0:T(4,128)} %bitcast.10, bf16[128,2048]{1,0:T(8,128)(2,1)} %tokens_ref.1, bf16[128,2048]{1,0:T(8,128)(2,1)} %grad_ref.1), custom_call_target="tpu_custom_call" | custom-call | bytes 6291456 | tf_op jit(solution)/shard_map/pallas_call | solution.py:353
  5.4 0.0 copy-start.5
  5.4 13.3 %all-to-all-start = ((bf16[64,8,4096]{2,1,0:T(8,128)(2,1)}), bf16[64,8,4096]{2,1,0:T(8,128)(2,1)}, u32[]{:S(2)}, u32[]{:S(2)}) async-start(bf16[64,8,4096]{2,1,0:T(8,128)(2,1)} %bitcast.8), calls=%async_computation | async-start | bytes 8388608 | tf_op jit(solution)/shard_map/all_to_all | solution.py:301
  18.7 0.0 copy-done.5
  18.7 0.0 copy-start.6
  18.7 0.0 copy-start.7
  18.7 0.1 constant_dynamic-update-slice_fusion.2
  18.8 1.1 copy-done.6
  19.8 0.1 constant_dynamic-update-slice_fusion.1
  19.9 0.2 copy-done.7
  20.1 0.1 constant_dynamic-update-slice_fusion
  20.1 2.8 %collective-permute-start.1 = (bf16[3,512,768]{2,1,0:T(8,128)(2,1)S(1)}, bf16[3,512,768]{2,1,0:T(8,128)(2,1)S(1)}, u32[]{:S(2)}, u32[]{:S(2)}) collective-permute-start(bf16[3,512,768]{2,1,0:T(8,128)(2,1)S(1)} %constant_dynamic-update-slice_fusion), channel_id=1, source_target_pairs={{0,192},{64,0},{128,64},{192,128},{1,193},{65,1},{129,65},{193,129... | collective-permute-start | bytes 7077896 | tf_op jit(solution)/shard_map/ppermute | solution.py:306
  22.9 0.0 collective-permute-start
  22.9 50.1 %collective-permute-done.1.above = bf16[3,512,768]{2,1,0:T(8,128)(2,1)S(1)} collective-permute-done((bf16[3,512,768]{2,1,0:T(8,128)(2,1)S(1)}, bf16[3,512,768]{2,1,0:T(8,128)(2,1)S(1)}, u32[]{:S(2)}, u32[]{:S(2)}) %collective-permute-start.1) | collective-permute-done | bytes 2359328 | tf_op jit(solution)/shard_map/ppermute | solution.py:306
  73.0 0.1 slice.25
  73.1 3.6 %collective-permute-start.3 = (bf16[3,256,768]{2,1,0:T(8,128)(2,1)S(1)}, bf16[3,256,768]{2,1,0:T(8,128)(2,1)S(1)}, u32[]{:S(2)}, u32[]{:S(2)}) collective-permute-start(bf16[3,256,768]{2,1,0:T(8,128)(2,1)S(1)} %slice.25), channel_id=1, source_target_pairs={{0,192},{64,0},{128,64},{192,128},{1,193},{65,1},{129,65},{193,129... | collective-permute-start | bytes 3538952 | tf_op jit(solution)/shard_map/ppermute | solution.py:306
  76.7 0.0 collective-permute-done.below
  76.7 0.1 slice.24
  76.8 0.0 copy-done.8
  76.8 0.3 collective-permute-start.2
  77.0 1.1 copy-done.9
  78.1 22.6 %collective-permute-done.3.far_b = bf16[3,256,768]{2,1,0:T(8,128)(2,1)S(1)} collective-permute-done((bf16[3,256,768]{2,1,0:T(8,128)(2,1)S(1)}, bf16[3,256,768]{2,1,0:T(8,128)(2,1)S(1)}, u32[]{:S(2)}, u32[]{:S(2)}) %collective-permute-start.3) | collective-permute-done | bytes 1179680 | tf_op jit(solution)/shard_map/ppermute | solution.py:306
  100.7 3.6 %collective-permute-done.2.far_a = bf16[3,256,768]{2,1,0:T(8,128)(2,1)} collective-permute-done((bf16[3,256,768]{2,1,0:T(8,128)(2,1)S(1)}, bf16[3,256,768]{2,1,0:T(8,128)(2,1)}, u32[]{:S(2)}, u32[]{:S(2)}) %collective-permute-start.2) | collective-permute-done | bytes 1179680 | tf_op jit(solution)/shard_map/ppermute | solution.py:306
  104.3 0.0 copy-done.10
  104.3 10.2 %all-to-all-done = bf16[64,8,4096]{2,1,0:T(8,128)(2,1)} async-done(((bf16[64,8,4096]{2,1,0:T(8,128)(2,1)}), bf16[64,8,4096]{2,1,0:T(8,128)(2,1)}, u32[]{:S(2)}, u32[]{:S(2)}) %all-to-all-start) | async-done | bytes 4194336 | tf_op jit(solution)/shard_map/all_to_all | solution.py:301
  114.5 15.0 %middle.1 = (bf16[512,4096]{1,0:T(8,128)(2,1)}, bf16[512,768]{1,0:T(8,128)(2,1)}, bf16[512,768]{1,0:T(8,128)(2,1)}, bf16[512,768]{1,0:T(8,128)(2,1)}) custom-call(s32[1]{0:T(128)} %bitcast.2.y_ref, bf16[512,4096]{1,0:T(8,128)(2,1)} %bitcast.4.rows_hbm.rows_ref, bf16[1,512,768]{2,1,0:T(8,128)(2,1)} %gate_w.1, bf16[1,512,768]{2,1,0:T(8,128)(2,1)} %up_w.1, ...), custom_call_target="tpu_custom_call" | custom-call | flops 9663676416 | bytes 20971520 | tf_op jit(solution)/shard_map/middle/pallas_call | solution.py:384
  129.5 0.0 copy-start.3
  129.5 0.0 copy-start.4
  129.5 6.1 %all-to-all-start.1 = ((bf16[64,8,4096]{2,1,0:T(8,128)(2,1)}), bf16[64,8,4096]{2,1,0:T(8,128)(2,1)}, u32[]{:S(2)}, u32[]{:S(2)}) async-start(bf16[64,8,4096]{2,1,0:T(8,128)(2,1)} %bitcast.7), calls=%async_computation.1 | async-start | bytes 8388608 | tf_op jit(solution)/shard_map/all_to_all | solution.py:301
  135.6 0.0 copy-done.3
  135.6 0.0 copy-done.4
  135.6 0.0 copy-start.2
  135.6 5.7 %shard_map.132 = (bf16[512,1536]{1,0:T(8,128)(2,1)S(1)}, bf16[512,1536]{1,0:T(8,128)(2,1)S(1)}, bf16[512,1536]{1,0:T(8,128)(2,1)S(1)}, bf16[256,1536]{1,0:T(8,128)(2,1)S(1)}, bf16[256,1536]{1,0:T(8,128)(2,1)S(1)}) custom-call(s32[1]{0:T(128)} %bitcast.2.y_ref, bf16[512,4096]{1,0:T(8,128)(2,1)} %bitcast.4.rows_hbm.rows_ref, bf16[512,768]{1,0:T(8,128)(2,1)S(1)} %copy-done.3, ...), custom_call_target="tpu_custom_call" | custom-call | flops 3221225472 | bytes 10485760 | tf_op jit(solution)/shard_map/pallas_call | solution.py:259
  141.4 1.4 collective-permute-start.4
  142.8 1.5 collective-permute-start.5
  144.3 0.0 copy-done.2
  144.3 4.0 %shard_map.134 = (bf16[512,768]{1,0:T(8,128)(2,1)S(1)}, bf16[512,768]{1,0:T(8,128)(2,1)S(1)}, bf16[512,768]{1,0:T(8,128)(2,1)S(1)}, bf16[256,768]{1,0:T(8,128)(2,1)S(1)}, bf16[256,768]{1,0:T(8,128)(2,1)S(1)}) custom-call(s32[1]{0:T(128)} %bitcast.2.y_ref, bf16[512,4096]{1,0:T(8,128)(2,1)} %bitcast.4.rows_hbm.rows_ref, bf16[512,768]{1,0:T(8,128)(2,1)S(1)} %copy-done.2), custom_call_target="tpu_custom_call" | custom-call | flops 1610612736 | bytes 7340032 | tf_op jit(solution)/shard_map/pallas_call | solution.py:259
  148.4 0.1 collective-permute-start.8
  148.4 2.7 %collective-permute-start.9 = (bf16[512,768]{1,0:T(8,128)(2,1)S(1)}, bf16[512,768]{1,0:T(8,128)(2,1)S(1)}, u32[]{:S(2)}, u32[]{:S(2)}) collective-permute-start(bf16[512,768]{1,0:T(8,128)(2,1)S(1)} %get-tuple-element.48), channel_id=1, source_target_pairs={{0,192},{64,0},{128,64},{192,128},{1,193},{65,1},{129,65},{193,129... | collective-permute-start | bytes 2359304 | tf_op jit(solution)/shard_map/ppermute | solution.py:306
  151.1 26.9 %collective-permute-done.4.up_ref = bf16[512,1536]{1,0:T(8,128)(2,1)S(1)} collective-permute-done((bf16[512,1536]{1,0:T(8,128)(2,1)S(1)}, bf16[512,1536]{1,0:T(8,128)(2,1)S(1)}, u32[]{:S(2)}, u32[]{:S(2)}) %collective-permute-start.4) | collective-permute-done | bytes 1572896 | tf_op jit(solution)/shard_map/ppermute | solution.py:306
  178.1 0.2 add_convert_fusion.1
  178.2 0.1 collective-permute-start.6
  178.4 0.0 collective-permute-done.5.dn_ref
  178.4 0.2 add_convert_fusion
  178.6 0.0 copy-start
  178.6 0.0 copy-start.1
  178.6 2.7 %collective-permute-start.7 = (bf16[256,1536]{1,0:T(8,128)(2,1)S(1)}, bf16[256,1536]{1,0:T(8,128)(2,1)S(1)}, u32[]{:S(2)}, u32[]{:S(2)}) collective-permute-start(bf16[256,1536]{1,0:T(8,128)(2,1)S(1)} %add_convert_fusion), channel_id=1, source_target_pairs={{0,192},{64,0},{128,64},{192,128},{1,193},{65,1},{129,65},{193,129... | collective-permute-start | bytes 2359304 | tf_op jit(solution)/shard_map/ppermute | solution.py:306
  181.3 13.7 %collective-permute-done.8.up_ref = bf16[512,768]{1,0:T(8,128)(2,1)S(1)} collective-permute-done((bf16[512,768]{1,0:T(8,128)(2,1)S(1)}, bf16[512,768]{1,0:T(8,128)(2,1)S(1)}, u32[]{:S(2)}, u32[]{:S(2)}) %collective-permute-start.8) | collective-permute-done | bytes 786464 | tf_op jit(solution)/shard_map/ppermute | solution.py:306
  195.0 0.1 add_convert_fusion.3
  195.1 0.1 collective-permute-start.10
  195.2 0.0 collective-permute-done.9.dn_ref
  195.2 0.1 add_convert_fusion.2
  195.3 2.7 %collective-permute-start.11 = (bf16[256,768]{1,0:T(8,128)(2,1)S(1)}, bf16[256,768]{1,0:T(8,128)(2,1)S(1)}, u32[]{:S(2)}, u32[]{:S(2)}) collective-permute-start(bf16[256,768]{1,0:T(8,128)(2,1)S(1)} %add_convert_fusion.2), channel_id=1, source_target_pairs={{0,192},{64,0},{128,64},{192,128},{1,193},{65,1},{129,65},{193,129... | collective-permute-start | bytes 1179656 | tf_op jit(solution)/shard_map/ppermute | solution.py:306
  198.0 0.0 copy-done
  198.0 0.0 copy-done.1
  198.0 0.3 shard_map.129
  198.4 21.9 %collective-permute-done.10.below_ref = bf16[256,768]{1,0:T(8,128)(2,1)S(1)} collective-permute-done((bf16[256,768]{1,0:T(8,128)(2,1)S(1)}, bf16[256,768]{1,0:T(8,128)(2,1)S(1)}, u32[]{:S(2)}, u32[]{:S(2)}) %collective-permute-start.10) | collective-permute-done | bytes 393248 | tf_op jit(solution)/shard_map/ppermute | solution.py:306
  220.3 0.0 collective-permute-done.11.above_ref
  220.3 1.4 shard_map.135
  221.7 0.0 collective-permute-done.6.below_ref
  221.7 0.0 collective-permute-done.7.above_ref
  221.7 1.9 shard_map.133
  223.6 7.8 %all-to-all-done.1 = bf16[64,8,4096]{2,1,0:T(8,128)(2,1)} async-done(((bf16[64,8,4096]{2,1,0:T(8,128)(2,1)}), bf16[64,8,4096]{2,1,0:T(8,128)(2,1)}, u32[]{:S(2)}, u32[]{:S(2)}) %all-to-all-start.1) | async-done | bytes 4194336 | tf_op jit(solution)/shard_map/all_to_all | solution.py:301
  231.5 4.0 %shard_map.131 = (bf16[128,2048]{1,0:T(8,128)(2,1)}, bf16[128,2048]{1,0:T(8,128)(2,1)}) custom-call(bf16[256,512]{1,0:T(8,128)(2,1)S(1)} %shard_map.130.pieces_ref, bf16[128,512]{1,0:T(8,128)(2,1)S(1)} %get-tuple-element.31.pick_ref, bf16[512,4096]{1,0:T(8,128)(2,1)} %bitcast.6.rows_ref), custom_call_target="tpu_custom_call" | custom-call | bytes 6291456 | tf_op jit(solution)/shard_map/pallas_call | solution.py:405
  (4 shorter events, 0.0 us)
Async XLA Ops:
  5.4 13.3 %copy-start.5 = (bf16[1,512,768]{2,1,0:T(8,128)(2,1)S(1)}, bf16[1,512,768]{2,1,0:T(8,128)(2,1)}, u32[]{:S(2)}) copy-start(bf16[1,512,768]{2,1,0:T(8,128)(2,1)} %gate_w.1) | copy-start | bytes 2359300
  5.4 109.2 %all-to-all-start = ((bf16[64,8,4096]{2,1,0:T(8,128)(2,1)}), bf16[64,8,4096]{2,1,0:T(8,128)(2,1)}, u32[]{:S(2)}, u32[]{:S(2)}) async-start(bf16[64,8,4096]{2,1,0:T(8,128)(2,1)} %bitcast.8), calls=%async_computation | async-start | bytes 8388608 | tf_op jit(solution)/shard_map/all_to_all | solution.py:301
  18.7 1.1 copy-start.6
  18.7 1.4 copy-start.7
  20.1 52.9 %collective-permute-start.1 = (bf16[3,512,768]{2,1,0:T(8,128)(2,1)S(1)}, bf16[3,512,768]{2,1,0:T(8,128)(2,1)S(1)}, u32[]{:S(2)}, u32[]{:S(2)}) collective-permute-start(bf16[3,512,768]{2,1,0:T(8,128)(2,1)S(1)} %constant_dynamic-update-slice_fusion), channel_id=1, source_target_pairs={{0,192},{64,0},{128,64},{192,128},{1,193},{65,1},{129,65},{193,129... | collective-permute-start | bytes 7077896 | tf_op jit(solution)/shard_map/ppermute | solution.py:306
  22.9 53.8 %collective-permute-start = (bf16[3,512,768]{2,1,0:T(8,128)(2,1)S(1)}, bf16[3,512,768]{2,1,0:T(8,128)(2,1)S(1)}, u32[]{:S(2)}, u32[]{:S(2)}) collective-permute-start(bf16[3,512,768]{2,1,0:T(8,128)(2,1)S(1)} %constant_dynamic-update-slice_fusion), channel_id=1, source_target_pairs={{0,64},{64,128},{128,192},{192,0},{1,65},{65,129},{129,193},{193,1... | collective-permute-start | bytes 7077896 | tf_op jit(solution)/shard_map/ppermute | solution.py:306
  73.0 3.8 %copy-start.8 = (bf16[3,512,768]{2,1,0:T(8,128)(2,1)}, bf16[3,512,768]{2,1,0:T(8,128)(2,1)S(1)}, u32[]{:S(2)}) copy-start(bf16[3,512,768]{2,1,0:T(8,128)(2,1)S(1)} %collective-permute-done.1.above) | copy-start | bytes 7077892
  73.1 27.6 %collective-permute-start.3 = (bf16[3,256,768]{2,1,0:T(8,128)(2,1)S(1)}, bf16[3,256,768]{2,1,0:T(8,128)(2,1)S(1)}, u32[]{:S(2)}, u32[]{:S(2)}) collective-permute-start(bf16[3,256,768]{2,1,0:T(8,128)(2,1)S(1)} %slice.25), channel_id=1, source_target_pairs={{0,192},{64,0},{128,64},{192,128},{1,193},{65,1},{129,65},{193,129... | collective-permute-start | bytes 3538952 | tf_op jit(solution)/shard_map/ppermute | solution.py:306
  76.7 1.4 copy-start.9
  76.8 27.5 %collective-permute-start.2 = (bf16[3,256,768]{2,1,0:T(8,128)(2,1)S(1)}, bf16[3,256,768]{2,1,0:T(8,128)(2,1)}, u32[]{:S(2)}, u32[]{:S(2)}) collective-permute-start(bf16[3,256,768]{2,1,0:T(8,128)(2,1)S(1)} %slice.24), channel_id=1, source_target_pairs={{0,64},{64,128},{128,192},{192,0},{1,65},{65,129},{129,193},{193,1... | collective-permute-start | bytes 3538952 | tf_op jit(solution)/shard_map/ppermute | solution.py:306
  100.7 3.6 %copy-start.10 = (bf16[3,256,768]{2,1,0:T(8,128)(2,1)}, bf16[3,256,768]{2,1,0:T(8,128)(2,1)S(1)}, u32[]{:S(2)}) copy-start(bf16[3,256,768]{2,1,0:T(8,128)(2,1)S(1)} %collective-permute-done.3.far_b) | copy-start | bytes 3538948
  129.5 6.1 %copy-start.3 = (bf16[512,768]{1,0:T(8,128)(2,1)S(1)}, bf16[512,768]{1,0:T(8,128)(2,1)}, u32[]{:S(2)}) copy-start(bf16[512,768]{1,0:T(8,128)(2,1)} %get-tuple-element.36.refs_0_) | copy-start | bytes 2359300
  129.5 6.1 %copy-start.4 = (bf16[512,768]{1,0:T(8,128)(2,1)S(1)}, bf16[512,768]{1,0:T(8,128)(2,1)}, u32[]{:S(2)}) copy-start(bf16[512,768]{1,0:T(8,128)(2,1)} %get-tuple-element.37.refs_1_) | copy-start | bytes 2359300
  129.5 101.9 %all-to-all-start.1 = ((bf16[64,8,4096]{2,1,0:T(8,128)(2,1)}), bf16[64,8,4096]{2,1,0:T(8,128)(2,1)}, u32[]{:S(2)}, u32[]{:S(2)}) async-start(bf16[64,8,4096]{2,1,0:T(8,128)(2,1)} %bitcast.7), calls=%async_computation.1 | async-start | bytes 8388608 | tf_op jit(solution)/shard_map/all_to_all | solution.py:301
  135.6 8.7 %copy-start.2 = (bf16[512,768]{1,0:T(8,128)(2,1)S(1)}, bf16[512,768]{1,0:T(8,128)(2,1)}, u32[]{:S(2)}) copy-start(bf16[512,768]{1,0:T(8,128)(2,1)} %get-tuple-element.45.refs_0_) | copy-start | bytes 2359300
  141.4 36.7 %collective-permute-start.4 = (bf16[512,1536]{1,0:T(8,128)(2,1)S(1)}, bf16[512,1536]{1,0:T(8,128)(2,1)S(1)}, u32[]{:S(2)}, u32[]{:S(2)}) collective-permute-start(bf16[512,1536]{1,0:T(8,128)(2,1)S(1)} %get-tuple-element.39), channel_id=1, source_target_pairs={{0,64},{64,128},{128,192},{192,0},{1,65},{65,129},{129,193},{193,1... | collective-permute-start | bytes 4718600 | tf_op jit(solution)/shard_map/ppermute | solution.py:306
  142.8 35.6 %collective-permute-start.5 = (bf16[512,1536]{1,0:T(8,128)(2,1)S(1)}, bf16[512,1536]{1,0:T(8,128)(2,1)S(1)}, u32[]{:S(2)}, u32[]{:S(2)}) collective-permute-start(bf16[512,1536]{1,0:T(8,128)(2,1)S(1)} %get-tuple-element.40), channel_id=1, source_target_pairs={{0,192},{64,0},{128,64},{192,128},{1,193},{65,1},{129,65},{193,129... | collective-permute-start | bytes 4718600 | tf_op jit(solution)/shard_map/ppermute | solution.py:306
  148.4 46.7 %collective-permute-start.8 = (bf16[512,768]{1,0:T(8,128)(2,1)S(1)}, bf16[512,768]{1,0:T(8,128)(2,1)S(1)}, u32[]{:S(2)}, u32[]{:S(2)}) collective-permute-start(bf16[512,768]{1,0:T(8,128)(2,1)S(1)} %get-tuple-element.47), channel_id=1, source_target_pairs={{0,64},{64,128},{128,192},{192,0},{1,65},{65,129},{129,193},{193,1... | collective-permute-start | bytes 2359304 | tf_op jit(solution)/shard_map/ppermute | solution.py:306
  148.4 46.8 %collective-permute-start.9 = (bf16[512,768]{1,0:T(8,128)(2,1)S(1)}, bf16[512,768]{1,0:T(8,128)(2,1)S(1)}, u32[]{:S(2)}, u32[]{:S(2)}) collective-permute-start(bf16[512,768]{1,0:T(8,128)(2,1)S(1)} %get-tuple-element.48), channel_id=1, source_target_pairs={{0,192},{64,0},{128,64},{192,128},{1,193},{65,1},{129,65},{193,129... | collective-permute-start | bytes 2359304 | tf_op jit(solution)/shard_map/ppermute | solution.py:306
  178.2 43.5 %collective-permute-start.6 = (bf16[256,1536]{1,0:T(8,128)(2,1)S(1)}, bf16[256,1536]{1,0:T(8,128)(2,1)S(1)}, u32[]{:S(2)}, u32[]{:S(2)}) collective-permute-start(bf16[256,1536]{1,0:T(8,128)(2,1)S(1)} %add_convert_fusion.1), channel_id=1, source_target_pairs={{0,64},{64,128},{128,192},{192,0},{1,65},{65,129},{129,193},{193,1... | collective-permute-start | bytes 2359304 | tf_op jit(solution)/shard_map/ppermute | solution.py:306
  178.6 19.5 %copy-start = (s32[3,128]{1,0:T(4,128)S(1)}, s32[3,128]{1,0:T(4,128)}, u32[]{:S(2)}) copy-start(s32[3,128]{1,0:T(4,128)} %get-tuple-element.28.place_ref) | copy-start | bytes 4612
  178.6 19.5 %copy-start.1 = (f32[3,128]{1,0:T(4,128)S(1)}, f32[3,128]{1,0:T(4,128)}, u32[]{:S(2)}) copy-start(f32[3,128]{1,0:T(4,128)} %get-tuple-element.29.gate_ref) | copy-start | bytes 4612
  178.6 43.1 %collective-permute-start.7 = (bf16[256,1536]{1,0:T(8,128)(2,1)S(1)}, bf16[256,1536]{1,0:T(8,128)(2,1)S(1)}, u32[]{:S(2)}, u32[]{:S(2)}) collective-permute-start(bf16[256,1536]{1,0:T(8,128)(2,1)S(1)} %add_convert_fusion), channel_id=1, source_target_pairs={{0,192},{64,0},{128,64},{192,128},{1,193},{65,1},{129,65},{193,129... | collective-permute-start | bytes 2359304 | tf_op jit(solution)/shard_map/ppermute | solution.py:306
  195.1 25.2 %collective-permute-start.10 = (bf16[256,768]{1,0:T(8,128)(2,1)S(1)}, bf16[256,768]{1,0:T(8,128)(2,1)S(1)}, u32[]{:S(2)}, u32[]{:S(2)}) collective-permute-start(bf16[256,768]{1,0:T(8,128)(2,1)S(1)} %add_convert_fusion.3), channel_id=1, source_target_pairs={{0,64},{64,128},{128,192},{192,0},{1,65},{65,129},{129,193},{193,1... | collective-permute-start | bytes 1179656 | tf_op jit(solution)/shard_map/ppermute | solution.py:306
  195.3 25.0 %collective-permute-start.11 = (bf16[256,768]{1,0:T(8,128)(2,1)S(1)}, bf16[256,768]{1,0:T(8,128)(2,1)S(1)}, u32[]{:S(2)}, u32[]{:S(2)}) collective-permute-start(bf16[256,768]{1,0:T(8,128)(2,1)S(1)} %add_convert_fusion.2), channel_id=1, source_target_pairs={{0,192},{64,0},{128,64},{192,128},{1,193},{65,1},{129,65},{193,129... | collective-permute-start | bytes 1179656 | tf_op jit(solution)/shard_map/ppermute | solution.py:306

commit v4 on v3

--- a/solution.py
+++ b/solution.py
@@ -284,15 +284,32 @@
         )
 
 
-def combine_kernel(pieces_ref, pick_ref, rows_ref, out_ref, grad_ref):
-    count, width = out_ref.shape
-    parts = jnp.dot(pieces_ref[...], rows_ref[:, :width], preferred_element_type=F32)
-    out_ref[...] = added(
+def combine_kernel(
+    pieces_ref, pick_ref, rows_hbm, out_hbm, grad_hbm, rows, out, grad, sem, out_sem
+):
+    count, width = out.shape
+    halves = [slice(0, width), slice(width, 2 * width)]
+    gets = [
+        pltpu.make_async_copy(rows_hbm.at[:, at], rows.at[:, at], sem.at[i])
+        for i, at in enumerate(halves)
+    ]
+    puts = [
+        pltpu.make_async_copy(out, out_hbm, out_sem.at[0]),
+        pltpu.make_async_copy(grad, grad_hbm, out_sem.at[1]),
+    ]
+    for get in gets:
+        get.start()
+    gets[0].wait()
+    parts = jnp.dot(pieces_ref[...], rows[:, :width], preferred_element_type=F32)
+    out[...] = added(
         [parts[at : at + count] for at in range(0, parts.shape[0], count)]
     ).astype(BF)
-    grad_ref[...] = jnp.dot(
-        pick_ref[...], rows_ref[:, width:], preferred_element_type=F32
-    ).astype(BF)
+    puts[0].start()
+    gets[1].wait()
+    grad[...] = jnp.dot(pick_ref[...], rows[:, width:], preferred_element_type=F32).astype(BF)
+    puts[1].start()
+    for put in puts:
+        put.wait()
 
 
 def move_rows(rows, members):
@@ -370,11 +387,7 @@
         limit=16 * 2**20,
     )(place, gates)
     pieces = whole(
-        split_kernel,
-        [shape_of((2 * count, slots), BF)],
-        1,
-        nbytes=2**20,
-        limit=16 * 2**20,
+        split_kernel, [shape_of((2 * count, slots), BF)], 1, nbytes=2**20, limit=16 * 2**20
     )(gated)[0]
 
     weights = [gate_weight, up_weight, down_weight]
@@ -402,12 +415,18 @@
 
     down_grad = ring_sum(1, *partials(y, moved, width, [hid], size))[0]
     gate_grad, up_grad = ring_sum(2, *partials(y, moved, 0, [grad_gate, grad_up], size))
-    output, token_grad = whole(
+    token_rows = shape_of((count, width), BF)
+    output, token_grad = pl.pallas_call(
         combine_kernel,
-        [shape_of((count, width), BF)] * 2,
-        3,
-        nbytes=6 * 2**20,
-        limit=16 * 2**20,
+        out_shape=[token_rows, token_rows],
+        in_specs=[VMEM, VMEM, any_space],
+        out_specs=[any_space, any_space],
+        scratch_shapes=[pltpu.VMEM((slots, 2 * width), BF)]
+        + [pltpu.VMEM((count, width), BF)] * 2
+        + [dma((2,)), dma((2,))],
+        compiler_params=pltpu.CompilerParams(vmem_limit_bytes=16 * 2**20),
+        cost_estimate=pl.CostEstimate(flops=0, bytes_accessed=6 * 2**20, transcendentals=0),
+        name="combine",
     )(pieces, pick, returned)
     return (output, token_grad, gate_grad, up_grad, down_grad)
 

time: 236 us -> 236 us (level)
  no operation moved by 1% of the time
where the time goes in v4:
time: 236 us; the launch traced here: 235 us
  waiting for transfers between devices  157 us (67%)
  starting transfers between devices  37.4 us (16%)
  Pallas kernels  36.7 us (16%)
  local copies, waits for them, and re-layouts  2.68 us (1%)
    ppermute x12, waiting for transfers between devices, shift(): return lax.ppermute(x, 'dp', [(i, (i + by) % 4) for i in range(4)])  139 us
    all_to_all x2, starting transfers between devices, move_rows(): lax.all_to_all(buffer, 'expert', split_axis=0, concat_axis=0, tiled=True)  19.4 us
    all_to_all x2, waiting for transfers between devices, move_rows(): lax.all_to_all(buffer, 'expert', split_axis=0, concat_axis=0, tiled=True)  18 us
    ppermute x12, starting transfers between devices, shift(): return lax.ppermute(x, 'dp', [(i, (i + by) % 4) for i in range(4)])  18 us
    pallas_call x1, Pallas kernels, shards(): pl.pallas_call(functools.partial(middle_kernel, 256), out_shape=[shape_of...  15 us
    pallas_call x2, Pallas kernels, partials(): whole(functools.partial(partial_kernel, len(acts), base), [full, full, fu...  9.77 us
    pallas_call x1, Pallas kernels, shards(): whole(functools.partial(send_kernel, members, capacity), [shape_of((slots...  4.73 us
  transfers between devices with their start and end apart: 14, of which 8 were waited for; matrix products, arithmetic and copies ran while one was open for 0% of the time, Pallas kernels for 6%

profile of v4, /device:TPU:1, one launch (start us, length us, event | category | flops | bytes accessed | tf_op | source)
XLA Modules:
  0.0 235.2 jit_solution(13566555064729618816)
XLA Ops:
  0.6 4.7 %shard_map.128 = (bf16[512,4096]{1,0:T(8,128)(2,1)}, s32[3,128]{1,0:T(4,128)}, f32[3,128]{1,0:T(4,128)}) custom-call(s32[2]{0:T(128)} %bucket_ref.1, f32[8,16]{1,0:T(8,128)} %table_ref.1, s32[3,128]{1,0:T(4,128)} %bitcast.9, s32[3,128]{1,0:T(4,128)} %bitcast.10, bf16[128,2048]{1,0:T(8,128)(2,1)} %tokens_ref.1, bf16[128,2048]{1,0:T(8,128)(2,1)} %grad_ref.1), custom_call_target="tpu_custom_call" | custom-call | bytes 6291456 | tf_op jit(solution)/shard_map/pallas_call | solution.py:370
  5.4 0.0 copy-start.5
  5.4 13.3 %all-to-all-start = ((bf16[64,8,4096]{2,1,0:T(8,128)(2,1)}), bf16[64,8,4096]{2,1,0:T(8,128)(2,1)}, u32[]{:S(2)}, u32[]{:S(2)}) async-start(bf16[64,8,4096]{2,1,0:T(8,128)(2,1)} %bitcast.8), calls=%async_computation | async-start | bytes 8388608 | tf_op jit(solution)/shard_map/all_to_all | solution.py:318
  18.7 0.0 copy-done.5
  18.7 0.0 copy-start.6
  18.7 0.0 copy-start.7
  18.7 0.1 constant_dynamic-update-slice_fusion.2
  18.8 1.1 copy-done.6
  19.8 0.1 constant_dynamic-update-slice_fusion.1
  19.9 0.2 copy-done.7
  20.1 0.1 constant_dynamic-update-slice_fusion
  20.1 2.8 %collective-permute-start.1 = (bf16[3,512,768]{2,1,0:T(8,128)(2,1)S(1)}, bf16[3,512,768]{2,1,0:T(8,128)(2,1)S(1)}, u32[]{:S(2)}, u32[]{:S(2)}) collective-permute-start(bf16[3,512,768]{2,1,0:T(8,128)(2,1)S(1)} %constant_dynamic-update-slice_fusion), channel_id=1, source_target_pairs={{0,192},{64,0},{128,64},{192,128},{1,193},{65,1},{129,65},{193,129... | collective-permute-start | bytes 7077896 | tf_op jit(solution)/shard_map/ppermute | solution.py:323
  22.9 0.0 collective-permute-start
  22.9 50.1 %collective-permute-done.1.above = bf16[3,512,768]{2,1,0:T(8,128)(2,1)S(1)} collective-permute-done((bf16[3,512,768]{2,1,0:T(8,128)(2,1)S(1)}, bf16[3,512,768]{2,1,0:T(8,128)(2,1)S(1)}, u32[]{:S(2)}, u32[]{:S(2)}) %collective-permute-start.1) | collective-permute-done | bytes 2359328 | tf_op jit(solution)/shard_map/ppermute | solution.py:323
  73.0 0.1 slice.25
  73.1 3.6 %collective-permute-start.3 = (bf16[3,256,768]{2,1,0:T(8,128)(2,1)S(1)}, bf16[3,256,768]{2,1,0:T(8,128)(2,1)S(1)}, u32[]{:S(2)}, u32[]{:S(2)}) collective-permute-start(bf16[3,256,768]{2,1,0:T(8,128)(2,1)S(1)} %slice.25), channel_id=1, source_target_pairs={{0,192},{64,0},{128,64},{192,128},{1,193},{65,1},{129,65},{193,129... | collective-permute-start | bytes 3538952 | tf_op jit(solution)/shard_map/ppermute | solution.py:323
  76.7 0.0 collective-permute-done.below
  76.7 0.1 slice.24
  76.8 0.0 copy-done.8
  76.8 0.3 collective-permute-start.2
  77.0 1.1 copy-done.9
  78.1 22.6 %collective-permute-done.3.far_b = bf16[3,256,768]{2,1,0:T(8,128)(2,1)S(1)} collective-permute-done((bf16[3,256,768]{2,1,0:T(8,128)(2,1)S(1)}, bf16[3,256,768]{2,1,0:T(8,128)(2,1)S(1)}, u32[]{:S(2)}, u32[]{:S(2)}) %collective-permute-start.3) | collective-permute-done | bytes 1179680 | tf_op jit(solution)/shard_map/ppermute | solution.py:323
  100.7 3.6 %collective-permute-done.2.far_a = bf16[3,256,768]{2,1,0:T(8,128)(2,1)} collective-permute-done((bf16[3,256,768]{2,1,0:T(8,128)(2,1)S(1)}, bf16[3,256,768]{2,1,0:T(8,128)(2,1)}, u32[]{:S(2)}, u32[]{:S(2)}) %collective-permute-start.2) | collective-permute-done | bytes 1179680 | tf_op jit(solution)/shard_map/ppermute | solution.py:323
  104.3 0.0 copy-done.10
  104.3 10.2 %all-to-all-done = bf16[64,8,4096]{2,1,0:T(8,128)(2,1)} async-done(((bf16[64,8,4096]{2,1,0:T(8,128)(2,1)}), bf16[64,8,4096]{2,1,0:T(8,128)(2,1)}, u32[]{:S(2)}, u32[]{:S(2)}) %all-to-all-start) | async-done | bytes 4194336 | tf_op jit(solution)/shard_map/all_to_all | solution.py:318
  114.5 15.0 %middle.1 = (bf16[512,4096]{1,0:T(8,128)(2,1)}, bf16[512,768]{1,0:T(8,128)(2,1)}, bf16[512,768]{1,0:T(8,128)(2,1)}, bf16[512,768]{1,0:T(8,128)(2,1)}) custom-call(s32[1]{0:T(128)} %bitcast.2.y_ref, bf16[512,4096]{1,0:T(8,128)(2,1)} %bitcast.4.rows_hbm.rows_ref, bf16[1,512,768]{2,1,0:T(8,128)(2,1)} %gate_w.1, bf16[1,512,768]{2,1,0:T(8,128)(2,1)} %up_w.1, ...), custom_call_target="tpu_custom_call" | custom-call | flops 9663676416 | bytes 20971520 | tf_op jit(solution)/shard_map/middle/pallas_call | solution.py:397
  129.5 0.0 copy-start.3
  129.5 0.0 copy-start.4
  129.5 6.1 %all-to-all-start.1 = ((bf16[64,8,4096]{2,1,0:T(8,128)(2,1)}), bf16[64,8,4096]{2,1,0:T(8,128)(2,1)}, u32[]{:S(2)}, u32[]{:S(2)}) async-start(bf16[64,8,4096]{2,1,0:T(8,128)(2,1)} %bitcast.7), calls=%async_computation.1 | async-start | bytes 8388608 | tf_op jit(solution)/shard_map/all_to_all | solution.py:318
  135.6 0.0 copy-done.3
  135.6 0.0 copy-done.4
  135.6 0.0 copy-start.2
  135.6 5.7 %shard_map.131 = (bf16[512,1536]{1,0:T(8,128)(2,1)S(1)}, bf16[512,1536]{1,0:T(8,128)(2,1)S(1)}, bf16[512,1536]{1,0:T(8,128)(2,1)S(1)}, bf16[256,1536]{1,0:T(8,128)(2,1)S(1)}, bf16[256,1536]{1,0:T(8,128)(2,1)S(1)}) custom-call(s32[1]{0:T(128)} %bitcast.2.y_ref, bf16[512,4096]{1,0:T(8,128)(2,1)} %bitcast.4.rows_hbm.rows_ref, bf16[512,768]{1,0:T(8,128)(2,1)S(1)} %copy-done.3, ...), custom_call_target="tpu_custom_call" | custom-call | flops 3221225472 | bytes 10485760 | tf_op jit(solution)/shard_map/pallas_call | solution.py:259
  141.4 1.4 collective-permute-start.4
  142.8 1.5 collective-permute-start.5
  144.3 0.0 copy-done.2
  144.3 4.0 %shard_map.133 = (bf16[512,768]{1,0:T(8,128)(2,1)S(1)}, bf16[512,768]{1,0:T(8,128)(2,1)S(1)}, bf16[512,768]{1,0:T(8,128)(2,1)S(1)}, bf16[256,768]{1,0:T(8,128)(2,1)S(1)}, bf16[256,768]{1,0:T(8,128)(2,1)S(1)}) custom-call(s32[1]{0:T(128)} %bitcast.2.y_ref, bf16[512,4096]{1,0:T(8,128)(2,1)} %bitcast.4.rows_hbm.rows_ref, bf16[512,768]{1,0:T(8,128)(2,1)S(1)} %copy-done.2), custom_call_target="tpu_custom_call" | custom-call | flops 1610612736 | bytes 7340032 | tf_op jit(solution)/shard_map/pallas_call | solution.py:259
  148.4 0.1 collective-permute-start.8
  148.4 2.7 %collective-permute-start.9 = (bf16[512,768]{1,0:T(8,128)(2,1)S(1)}, bf16[512,768]{1,0:T(8,128)(2,1)S(1)}, u32[]{:S(2)}, u32[]{:S(2)}) collective-permute-start(bf16[512,768]{1,0:T(8,128)(2,1)S(1)} %get-tuple-element.48), channel_id=1, source_target_pairs={{0,192},{64,0},{128,64},{192,128},{1,193},{65,1},{129,65},{193,129... | collective-permute-start | bytes 2359304 | tf_op jit(solution)/shard_map/ppermute | solution.py:323
  151.1 26.9 %collective-permute-done.4.up_ref = bf16[512,1536]{1,0:T(8,128)(2,1)S(1)} collective-permute-done((bf16[512,1536]{1,0:T(8,128)(2,1)S(1)}, bf16[512,1536]{1,0:T(8,128)(2,1)S(1)}, u32[]{:S(2)}, u32[]{:S(2)}) %collective-permute-start.4) | collective-permute-done | bytes 1572896 | tf_op jit(solution)/shard_map/ppermute | solution.py:323
  178.1 0.2 add_convert_fusion.1
  178.2 0.1 collective-permute-start.6
  178.4 0.0 collective-permute-done.5.dn_ref
  178.4 0.2 add_convert_fusion
  178.6 0.0 copy-start
  178.6 0.0 copy-start.1
  178.6 2.7 %collective-permute-start.7 = (bf16[256,1536]{1,0:T(8,128)(2,1)S(1)}, bf16[256,1536]{1,0:T(8,128)(2,1)S(1)}, u32[]{:S(2)}, u32[]{:S(2)}) collective-permute-start(bf16[256,1536]{1,0:T(8,128)(2,1)S(1)} %add_convert_fusion), channel_id=1, source_target_pairs={{0,192},{64,0},{128,64},{192,128},{1,193},{65,1},{129,65},{193,129... | collective-permute-start | bytes 2359304 | tf_op jit(solution)/shard_map/ppermute | solution.py:323
  181.3 13.7 %collective-permute-done.8.up_ref = bf16[512,768]{1,0:T(8,128)(2,1)S(1)} collective-permute-done((bf16[512,768]{1,0:T(8,128)(2,1)S(1)}, bf16[512,768]{1,0:T(8,128)(2,1)S(1)}, u32[]{:S(2)}, u32[]{:S(2)}) %collective-permute-start.8) | collective-permute-done | bytes 786464 | tf_op jit(solution)/shard_map/ppermute | solution.py:323
  195.0 0.1 add_convert_fusion.3
  195.1 0.1 collective-permute-start.10
  195.2 0.0 collective-permute-done.9.dn_ref
  195.2 0.1 add_convert_fusion.2
  195.3 2.7 %collective-permute-start.11 = (bf16[256,768]{1,0:T(8,128)(2,1)S(1)}, bf16[256,768]{1,0:T(8,128)(2,1)S(1)}, u32[]{:S(2)}, u32[]{:S(2)}) collective-permute-start(bf16[256,768]{1,0:T(8,128)(2,1)S(1)} %add_convert_fusion.2), channel_id=1, source_target_pairs={{0,192},{64,0},{128,64},{192,128},{1,193},{65,1},{129,65},{193,129... | collective-permute-start | bytes 1179656 | tf_op jit(solution)/shard_map/ppermute | solution.py:323
  198.0 0.0 copy-done
  198.0 0.0 copy-done.1
  198.0 0.3 shard_map.129
  198.4 21.9 %collective-permute-done.10.below_ref = bf16[256,768]{1,0:T(8,128)(2,1)S(1)} collective-permute-done((bf16[256,768]{1,0:T(8,128)(2,1)S(1)}, bf16[256,768]{1,0:T(8,128)(2,1)S(1)}, u32[]{:S(2)}, u32[]{:S(2)}) %collective-permute-start.10) | collective-permute-done | bytes 393248 | tf_op jit(solution)/shard_map/ppermute | solution.py:323
  220.3 0.0 collective-permute-done.11.above_ref
  220.3 1.4 shard_map.134
  221.7 0.0 collective-permute-done.6.below_ref
  221.7 0.0 collective-permute-done.7.above_ref
  221.7 1.9 shard_map.132
  223.6 7.8 %all-to-all-done.1 = bf16[64,8,4096]{2,1,0:T(8,128)(2,1)} async-done(((bf16[64,8,4096]{2,1,0:T(8,128)(2,1)}), bf16[64,8,4096]{2,1,0:T(8,128)(2,1)}, u32[]{:S(2)}, u32[]{:S(2)}) %all-to-all-start.1) | async-done | bytes 4194336 | tf_op jit(solution)/shard_map/all_to_all | solution.py:318
  231.5 3.6 %combine.1 = (bf16[128,2048]{1,0:T(8,128)(2,1)}, bf16[128,2048]{1,0:T(8,128)(2,1)}) custom-call(bf16[256,512]{1,0:T(8,128)(2,1)S(1)} %shard_map.130.pieces_ref, bf16[128,512]{1,0:T(8,128)(2,1)S(1)} %get-tuple-element.31.pick_ref, bf16[512,4096]{1,0:T(8,128)(2,1)} %bitcast.6.rows_hbm), custom_call_target="tpu_custom_call" | custom-call | bytes 6291456 | tf_op jit(solution)/shard_map/combine/pallas_call | solution.py:419
  (4 shorter events, 0.0 us)
Async XLA Ops:
  5.4 13.3 %copy-start.5 = (bf16[1,512,768]{2,1,0:T(8,128)(2,1)S(1)}, bf16[1,512,768]{2,1,0:T(8,128)(2,1)}, u32[]{:S(2)}) copy-start(bf16[1,512,768]{2,1,0:T(8,128)(2,1)} %gate_w.1) | copy-start | bytes 2359300
  5.4 109.2 %all-to-all-start = ((bf16[64,8,4096]{2,1,0:T(8,128)(2,1)}), bf16[64,8,4096]{2,1,0:T(8,128)(2,1)}, u32[]{:S(2)}, u32[]{:S(2)}) async-start(bf16[64,8,4096]{2,1,0:T(8,128)(2,1)} %bitcast.8), calls=%async_computation | async-start | bytes 8388608 | tf_op jit(solution)/shard_map/all_to_all | solution.py:318
  18.7 1.1 copy-start.6
  18.7 1.4 copy-start.7
  20.1 52.9 %collective-permute-start.1 = (bf16[3,512,768]{2,1,0:T(8,128)(2,1)S(1)}, bf16[3,512,768]{2,1,0:T(8,128)(2,1)S(1)}, u32[]{:S(2)}, u32[]{:S(2)}) collective-permute-start(bf16[3,512,768]{2,1,0:T(8,128)(2,1)S(1)} %constant_dynamic-update-slice_fusion), channel_id=1, source_target_pairs={{0,192},{64,0},{128,64},{192,128},{1,193},{65,1},{129,65},{193,129... | collective-permute-start | bytes 7077896 | tf_op jit(solution)/shard_map/ppermute | solution.py:323
  22.9 53.8 %collective-permute-start = (bf16[3,512,768]{2,1,0:T(8,128)(2,1)S(1)}, bf16[3,512,768]{2,1,0:T(8,128)(2,1)S(1)}, u32[]{:S(2)}, u32[]{:S(2)}) collective-permute-start(bf16[3,512,768]{2,1,0:T(8,128)(2,1)S(1)} %constant_dynamic-update-slice_fusion), channel_id=1, source_target_pairs={{0,64},{64,128},{128,192},{192,0},{1,65},{65,129},{129,193},{193,1... | collective-permute-start | bytes 7077896 | tf_op jit(solution)/shard_map/ppermute | solution.py:323
  73.0 3.8 %copy-start.8 = (bf16[3,512,768]{2,1,0:T(8,128)(2,1)}, bf16[3,512,768]{2,1,0:T(8,128)(2,1)S(1)}, u32[]{:S(2)}) copy-start(bf16[3,512,768]{2,1,0:T(8,128)(2,1)S(1)} %collective-permute-done.1.above) | copy-start | bytes 7077892
  73.1 27.6 %collective-permute-start.3 = (bf16[3,256,768]{2,1,0:T(8,128)(2,1)S(1)}, bf16[3,256,768]{2,1,0:T(8,128)(2,1)S(1)}, u32[]{:S(2)}, u32[]{:S(2)}) collective-permute-start(bf16[3,256,768]{2,1,0:T(8,128)(2,1)S(1)} %slice.25), channel_id=1, source_target_pairs={{0,192},{64,0},{128,64},{192,128},{1,193},{65,1},{129,65},{193,129... | collective-permute-start | bytes 3538952 | tf_op jit(solution)/shard_map/ppermute | solution.py:323
  76.7 1.4 copy-start.9
  76.8 27.5 %collective-permute-start.2 = (bf16[3,256,768]{2,1,0:T(8,128)(2,1)S(1)}, bf16[3,256,768]{2,1,0:T(8,128)(2,1)}, u32[]{:S(2)}, u32[]{:S(2)}) collective-permute-start(bf16[3,256,768]{2,1,0:T(8,128)(2,1)S(1)} %slice.24), channel_id=1, source_target_pairs={{0,64},{64,128},{128,192},{192,0},{1,65},{65,129},{129,193},{193,1... | collective-permute-start | bytes 3538952 | tf_op jit(solution)/shard_map/ppermute | solution.py:323
  100.7 3.6 %copy-start.10 = (bf16[3,256,768]{2,1,0:T(8,128)(2,1)}, bf16[3,256,768]{2,1,0:T(8,128)(2,1)S(1)}, u32[]{:S(2)}) copy-start(bf16[3,256,768]{2,1,0:T(8,128)(2,1)S(1)} %collective-permute-done.3.far_b) | copy-start | bytes 3538948
  129.5 6.1 %copy-start.3 = (bf16[512,768]{1,0:T(8,128)(2,1)S(1)}, bf16[512,768]{1,0:T(8,128)(2,1)}, u32[]{:S(2)}) copy-start(bf16[512,768]{1,0:T(8,128)(2,1)} %get-tuple-element.36.refs_0_) | copy-start | bytes 2359300
  129.5 6.1 %copy-start.4 = (bf16[512,768]{1,0:T(8,128)(2,1)S(1)}, bf16[512,768]{1,0:T(8,128)(2,1)}, u32[]{:S(2)}) copy-start(bf16[512,768]{1,0:T(8,128)(2,1)} %get-tuple-element.37.refs_1_) | copy-start | bytes 2359300
  129.5 101.9 %all-to-all-start.1 = ((bf16[64,8,4096]{2,1,0:T(8,128)(2,1)}), bf16[64,8,4096]{2,1,0:T(8,128)(2,1)}, u32[]{:S(2)}, u32[]{:S(2)}) async-start(bf16[64,8,4096]{2,1,0:T(8,128)(2,1)} %bitcast.7), calls=%async_computation.1 | async-start | bytes 8388608 | tf_op jit(solution)/shard_map/all_to_all | solution.py:318
  135.6 8.7 %copy-start.2 = (bf16[512,768]{1,0:T(8,128)(2,1)S(1)}, bf16[512,768]{1,0:T(8,128)(2,1)}, u32[]{:S(2)}) copy-start(bf16[512,768]{1,0:T(8,128)(2,1)} %get-tuple-element.45.refs_0_) | copy-start | bytes 2359300
  141.4 36.7 %collective-permute-start.4 = (bf16[512,1536]{1,0:T(8,128)(2,1)S(1)}, bf16[512,1536]{1,0:T(8,128)(2,1)S(1)}, u32[]{:S(2)}, u32[]{:S(2)}) collective-permute-start(bf16[512,1536]{1,0:T(8,128)(2,1)S(1)} %get-tuple-element.39), channel_id=1, source_target_pairs={{0,64},{64,128},{128,192},{192,0},{1,65},{65,129},{129,193},{193,1... | collective-permute-start | bytes 4718600 | tf_op jit(solution)/shard_map/ppermute | solution.py:323
  142.8 35.6 %collective-permute-start.5 = (bf16[512,1536]{1,0:T(8,128)(2,1)S(1)}, bf16[512,1536]{1,0:T(8,128)(2,1)S(1)}, u32[]{:S(2)}, u32[]{:S(2)}) collective-permute-start(bf16[512,1536]{1,0:T(8,128)(2,1)S(1)} %get-tuple-element.40), channel_id=1, source_target_pairs={{0,192},{64,0},{128,64},{192,128},{1,193},{65,1},{129,65},{193,129... | collective-permute-start | bytes 4718600 | tf_op jit(solution)/shard_map/ppermute | solution.py:323
  148.4 46.7 %collective-permute-start.8 = (bf16[512,768]{1,0:T(8,128)(2,1)S(1)}, bf16[512,768]{1,0:T(8,128)(2,1)S(1)}, u32[]{:S(2)}, u32[]{:S(2)}) collective-permute-start(bf16[512,768]{1,0:T(8,128)(2,1)S(1)} %get-tuple-element.47), channel_id=1, source_target_pairs={{0,64},{64,128},{128,192},{192,0},{1,65},{65,129},{129,193},{193,1... | collective-permute-start | bytes 2359304 | tf_op jit(solution)/shard_map/ppermute | solution.py:323
  148.4 46.8 %collective-permute-start.9 = (bf16[512,768]{1,0:T(8,128)(2,1)S(1)}, bf16[512,768]{1,0:T(8,128)(2,1)S(1)}, u32[]{:S(2)}, u32[]{:S(2)}) collective-permute-start(bf16[512,768]{1,0:T(8,128)(2,1)S(1)} %get-tuple-element.48), channel_id=1, source_target_pairs={{0,192},{64,0},{128,64},{192,128},{1,193},{65,1},{129,65},{193,129... | collective-permute-start | bytes 2359304 | tf_op jit(solution)/shard_map/ppermute | solution.py:323
  178.2 43.5 %collective-permute-start.6 = (bf16[256,1536]{1,0:T(8,128)(2,1)S(1)}, bf16[256,1536]{1,0:T(8,128)(2,1)S(1)}, u32[]{:S(2)}, u32[]{:S(2)}) collective-permute-start(bf16[256,1536]{1,0:T(8,128)(2,1)S(1)} %add_convert_fusion.1), channel_id=1, source_target_pairs={{0,64},{64,128},{128,192},{192,0},{1,65},{65,129},{129,193},{193,1... | collective-permute-start | bytes 2359304 | tf_op jit(solution)/shard_map/ppermute | solution.py:323
  178.6 19.5 %copy-start = (s32[3,128]{1,0:T(4,128)S(1)}, s32[3,128]{1,0:T(4,128)}, u32[]{:S(2)}) copy-start(s32[3,128]{1,0:T(4,128)} %get-tuple-element.28.place_ref) | copy-start | bytes 4612
  178.6 19.5 %copy-start.1 = (f32[3,128]{1,0:T(4,128)S(1)}, f32[3,128]{1,0:T(4,128)}, u32[]{:S(2)}) copy-start(f32[3,128]{1,0:T(4,128)} %get-tuple-element.29.gate_ref) | copy-start | bytes 4612
  178.6 43.1 %collective-permute-start.7 = (bf16[256,1536]{1,0:T(8,128)(2,1)S(1)}, bf16[256,1536]{1,0:T(8,128)(2,1)S(1)}, u32[]{:S(2)}, u32[]{:S(2)}) collective-permute-start(bf16[256,1536]{1,0:T(8,128)(2,1)S(1)} %add_convert_fusion), channel_id=1, source_target_pairs={{0,192},{64,0},{128,64},{192,128},{1,193},{65,1},{129,65},{193,129... | collective-permute-start | bytes 2359304 | tf_op jit(solution)/shard_map/ppermute | solution.py:323
  195.1 25.2 %collective-permute-start.10 = (bf16[256,768]{1,0:T(8,128)(2,1)S(1)}, bf16[256,768]{1,0:T(8,128)(2,1)S(1)}, u32[]{:S(2)}, u32[]{:S(2)}) collective-permute-start(bf16[256,768]{1,0:T(8,128)(2,1)S(1)} %add_convert_fusion.3), channel_id=1, source_target_pairs={{0,64},{64,128},{128,192},{192,0},{1,65},{65,129},{129,193},{193,1... | collective-permute-start | bytes 1179656 | tf_op jit(solution)/shard_map/ppermute | solution.py:323
  195.3 25.0 %collective-permute-start.11 = (bf16[256,768]{1,0:T(8,128)(2,1)S(1)}, bf16[256,768]{1,0:T(8,128)(2,1)S(1)}, u32[]{:S(2)}, u32[]{:S(2)}) collective-permute-start(bf16[256,768]{1,0:T(8,128)(2,1)S(1)} %add_convert_fusion.2), channel_id=1, source_target_pairs={{0,192},{64,0},{128,64},{192,128},{1,193},{65,1},{129,65},{193,129... | collective-permute-start | bytes 1179656 | tf_op jit(solution)/shard_map/ppermute | solution.py:323
